TPU v7x, 32 devices: a whole 2x2x4 slice. The times are simulated.
32 devices in a mesh: spec: 4 (over z), space: 8 (over y, x, core).
Axes of the slice: x: 2, y: 2, z: 4, core: 2. Of those that a mesh axis runs over, the one named last changes fastest.
Arguments:
- spectrum: bfloat16 [1296, 128, 256], P('spec', 'space'), may hold values from 0.049804688 to 1
- land_sea: int32 [128, 256], P('space'), may hold values from 0 to 1, as said below
- owners: int32 [4], replicated, may hold values from 0 to 3, each once
- proj_weight: bfloat16 [512, 1296], replicated, may hold values from -0.15625 to 0.15625
- back_weight: bfloat16 [1296, 512], replicated, may hold values from -0.25 to 0.25
- ocean_vel: float32 [2, 32, 4, 8, 1024], P(None, None, 'spec', 'space'), may hold values from -4 to 4
- mixing: float32 [32, 4, 8, 1024], P(None, 'spec', 'space'), may hold values from 0.03 to 0.25
- active_layers: int32 [4, 8, 1024], P('spec', 'space'), may hold values from 1 to 32
Outputs:
- new_spectrum: bfloat16 [1296, 128, 256], P('spec', 'space')
- new_ocean: float32 [2, 32, 4, 8, 1024], P(None, None, 'spec', 'space')
Inputs may be any that keep to these rules, and one draw needn't show every extreme that they name: `land_sea`: in every aligned block of 4 rows (1024 points) at most 768 points are sea; some block has exactly 768. `owners`: A permutation: the ocean slots of a strip cover its 4 blocks once each.
All inputs are finite; a program needn't handle non-finite values.
Results may differ from a plain program's by a relative error of at most 0.0064.
Values may be sent and summed in bfloat16 or wider, within the bound.
A program may use at most 64 MiB of HBM per device.

v0:
```python
import math

import jax
import jax.numpy as jnp
from jax import lax
from jax.sharding import PartitionSpec as P

NDIR = 36
NFREQ = 36
K = 1296
LAYERS = 32
STEPS = 2


courant_scale = 0.5
current_scale = 0.15
source_step = 0.25
coriolis = 0.3
stress_scale = 0.5
drift_scale = 4.0


def with_halo(cells, sides, width):
    for axis, dim in sides:
        count = lax.axis_size(axis)
        ends = count - 1
        head = lax.slice_in_dim(cells, 0, width, axis=dim)
        tail = lax.slice_in_dim(cells, cells.shape[dim] - width, cells.shape[dim], axis=dim)
        cells = jnp.concatenate(
            [
                lax.ppermute(tail, axis, [(i, (i + 1) % count) for i in range(ends)]),
                cells,
                lax.ppermute(head, axis, [((i + 1) % count, i) for i in range(ends)]),
            ],
            axis=dim,
        )
    return cells


def component_tables():
    component = jnp.arange(K, dtype=jnp.int32)
    frequency = component // NDIR
    direction = component % NDIR
    angle = (direction.astype(jnp.float32) + 0.5) * (2.0 * math.pi / NDIR)
    group_speed = courant_scale * jnp.exp(-2.0 * frequency.astype(jnp.float32) / NFREQ)
    eastward = (4 * direction + 2 < NDIR) | (4 * direction + 2 > 3 * NDIR)
    northward = 2 * direction + 1 < NDIR
    return (group_speed * jnp.cos(angle), group_speed * jnp.sin(angle), eastward, northward)


def coupling_tables():
    component = jnp.arange(K, dtype=jnp.int32)
    frequency = (component // NDIR).astype(jnp.float32)
    direction = (component % NDIR).astype(jnp.float32)
    angle = (direction + 0.5) * (2.0 * math.pi / NDIR)
    wavenum = 0.02 * jnp.exp(6.0 * frequency / NFREQ)
    depth = jnp.arange(LAYERS, dtype=jnp.float32)[:, None] + 0.5
    decay_rows = wavenum[None, :] ** 1.5 * jnp.exp(-2.0 * wavenum[None, :] * depth)
    decay_rows = decay_rows / jnp.sqrt(jnp.sum(decay_rows * decay_rows, axis=1, keepdims=True))
    drift_rows = drift_scale * jnp.concatenate(
        [decay_rows * jnp.cos(angle)[None, :], decay_rows * jnp.sin(angle)[None, :]], 0
    )
    stress = wavenum / jnp.sqrt(jnp.sum(wavenum * wavenum))
    stress_rows = -stress_scale * jnp.stack([stress * jnp.cos(angle), stress * jnp.sin(angle)], 0)
    return (drift_rows, stress_rows)


def face_difference(padded, forward_mask, axis):
    face_count = padded.shape[axis] - 4
    cell_before = lax.slice_in_dim(padded, 0, face_count + 1, axis=axis)
    cell_left = lax.slice_in_dim(padded, 1, face_count + 2, axis=axis)
    cell_right = lax.slice_in_dim(padded, 2, face_count + 3, axis=axis)
    cell_after = lax.slice_in_dim(padded, 3, face_count + 4, axis=axis)
    forward = (5.0 * cell_left + 2.0 * cell_right - cell_before) / 6.0
    backward = (2.0 * cell_left + 5.0 * cell_right - cell_after) / 6.0
    face_flux = jnp.where(forward_mask, forward, backward)
    return lax.slice_in_dim(face_flux, 1, face_count + 1, axis=axis) - lax.slice_in_dim(
        face_flux, 0, face_count, axis=axis
    )


def propagate(spectral_state, land_mask, currents, speed_east, speed_north, eastward, northward):
    masked = spectral_state.astype(jnp.float32) * land_mask
    flux_east = (speed_east[:, None, None] + current_scale * currents[0]) * masked
    padded_east = with_halo(flux_east, (("space", 1),), 2)
    flux_north = (speed_north[:, None, None] + current_scale * currents[1]) * masked
    padded_north = jnp.pad(flux_north, ((0, 0), (0, 0), (2, 2)))
    advected = (
        masked
        - face_difference(padded_east, eastward[:, None, None], 1)
        - face_difference(padded_north, northward[:, None, None], 2)
    )
    return (advected * land_mask).astype(jnp.bfloat16)


def source_block(drift_block, proj_weight, back_weight, drift_rows, stress_rows):
    projected = jnp.dot(proj_weight, drift_block, preferred_element_type=jnp.float32)
    cubed = (projected * projected * projected).astype(jnp.bfloat16)
    transfer = jnp.dot(back_weight, cubed, preferred_element_type=jnp.float32)
    updated = drift_block.astype(jnp.float32) + source_step * transfer
    payload = jnp.concatenate(
        [
            jnp.dot(drift_rows, updated, precision=lax.Precision.HIGHEST),
            jnp.dot(stress_rows, transfer, precision=lax.Precision.HIGHEST),
        ],
        0,
    )
    return (updated.astype(jnp.bfloat16), payload)


def ocean_step(velocity, payload, mixing, active):
    layer_index = lax.broadcasted_iota(jnp.int32, mixing.shape, 0)
    live_layer = (layer_index < active[None]).astype(jnp.float32)
    bottom = (layer_index == active[None] - 1).astype(jnp.float32)
    surface = (layer_index == 0).astype(jnp.float32)
    upper_mix = mixing[:-1] * live_layer[1:]

    def mixed(field):
        between = upper_mix * (field[:-1] - field[1:])
        inflow = jnp.concatenate([jnp.zeros_like(between[:1]), between], 0)
        outflow = jnp.concatenate([between, jnp.zeros_like(between[:1])], 0)
        return inflow - outflow - mixing * bottom * field

    east_vel = velocity[0]
    north_vel = velocity[1]
    drift_east = payload[:LAYERS]
    drift_north = payload[LAYERS : 2 * LAYERS]
    stress_east = payload[2 * LAYERS][None]
    stress_north = payload[2 * LAYERS + 1][None]
    new_east = live_layer * (
        east_vel + coriolis * (north_vel + drift_north) + mixed(east_vel) + surface * stress_east
    )
    new_north = live_layer * (
        north_vel - coriolis * (east_vel + drift_east) + mixed(north_vel) + surface * stress_north
    )
    return jnp.stack([new_east, new_north], 0)


def body(spectrum, land_sea, owners, proj_weight, back_weight, ocean_vel, mixing, active_layers):
    local_comps, strip_rows, strip_cols = spectrum.shape
    slot_count = lax.axis_size("spec")
    block_rows = strip_rows // slot_count
    block_points = block_rows * strip_cols
    spec_index = lax.axis_index("spec")
    first_comp = spec_index * local_comps
    speed_east, speed_north, eastward, northward = component_tables()
    speed_east = lax.dynamic_slice_in_dim(speed_east, first_comp, local_comps)
    speed_north = lax.dynamic_slice_in_dim(speed_north, first_comp, local_comps)
    eastward = lax.dynamic_slice_in_dim(eastward, first_comp, local_comps)
    northward = lax.dynamic_slice_in_dim(northward, first_comp, local_comps)
    drift_rows, stress_rows = coupling_tables()
    land_mask = land_sea.astype(jnp.float32)
    inverse = jnp.argsort(owners)
    velocity = ocean_vel.reshape(2, LAYERS, block_points)
    mixing_local = mixing.reshape(LAYERS, block_points)
    active = active_layers.reshape(block_points)
    spectral_state = spectrum
    for step_index in range(STEPS):
        surface = velocity[:, 0][:, None, :]
        gathered = lax.all_gather(surface, "spec", axis=1, tiled=True)
        currents = gathered[:, inverse].reshape(2, strip_rows, strip_cols)
        drifted = propagate(
            spectral_state, land_mask, currents, speed_east, speed_north, eastward, northward
        )
        blocks = drifted.reshape(local_comps, slot_count, block_points)
        blocks = blocks[:, owners]
        updated, payload = source_block(
            lax.all_to_all(blocks, "spec", split_axis=1, concat_axis=0, tiled=True)[:, 0, :],
            proj_weight,
            back_weight,
            drift_rows,
            stress_rows,
        )
        returned = lax.all_to_all(
            updated[:, None, :], "spec", split_axis=0, concat_axis=1, tiled=True
        )
        returned, payload = (returned, payload[:, None, :])
        returned = returned[:, inverse]
        spectral_state = returned.reshape(local_comps, strip_rows, strip_cols)
        payload = payload[:, 0, :]
        velocity = ocean_step(velocity, payload, mixing_local, active)
    return (spectral_state, velocity.reshape(ocean_vel.shape))


def solution(mesh):
    placed = (
        P("spec", "space", None),
        P("space", None),
        P(),
        P(),
        P(),
        P(None, None, "spec", "space", None),
        P(None, "spec", "space", None),
        P("spec", "space", None),
    )
    return jax.shard_map(
        body,
        mesh=mesh,
        in_specs=placed,
        out_specs=(P("spec", "space", None), P(None, None, "spec", "space", None)),
        check_vma=False,
    )
```

profile of v0, /device:TPU:2, one launch (start us, length us, event | category | flops | bytes accessed | tf_op | source)
XLA Modules:
  0.0 600.6 jit_solution(2278979046440001699)
XLA Ops:
  4.2 13.4 %all_gather.6 = f32[2,4,1024]{2,0,1:T(2,128)S(1)} all-gather(f32[2,1,1024]{2,0,1:T(2,128)S(1)} %slice.257), channel_id=1, replica_groups=mesh['spec'=4,'space'=8] {'spec'}, dimensions={1}, use_global_device_ids=true | all-gather | bytes 40960 | tf_op jit(solution)/shard_map/all_gather | solution.py:160
  23.5 3.6 collective-permute-start.1
  27.3 6.9 %fusion.2 = f32[324,16,257]{2,1,0:T(8,128)S(1)} fusion(f32[324,16,256]{2,1,0:T(8,128)S(1)} %get-tuple-element.25, pred[324]{0:T(512)(128)(4,1)S(1)} %get-tuple-element.47), kind=kLoop, calls=%fused_computation.16 | loop fusion | flops 14655168 | bytes 10637892 | tf_op jit(solution)/shard_map/jit(_where)/select_n | solution.py:76
  34.2 5.4 collective-permute-done.1
  39.7 7.0 %fusion.17 = f32[324,17,256]{2,1,0:T(8,128)S(1)} fusion(f32[324,2,256]{2,1,0:T(2,128)S(1)} %collective-permute-done.1, f32[324,16,256]{2,1,0:T(8,128)S(1)} %get-tuple-element.24, f32[324,2,256]{2,1,0:T(2,128)S(1)} %collective-permute-done, pred[324]{0:T(512)(128)(4,1)S(1)} %get-tuple-element.46), kind=kLoop, calls=%fused_computation.36 | loop fusion | flops 21150720 | bytes 12276036 | tf_op jit(solution)/shard_map/jit(_where)/select_n | solution.py:76
  46.7 3.4 fusion.26
  50.0 6.1 %reshape.194 = bf16[324,4,1024]{2,1,0:T(4,128)(2,1)} reshape(bf16[324,16,256]{2,1,0:T(8,128)(2,1)} %fusion.26) | data formatting | bytes 5308416 | tf_op jit(solution)/shard_map/reshape | solution.py:165
  56.1 4.1 copy.61
  60.2 4.0 gather_fusion.1
  64.2 66.7 %all_to_all.66 = bf16[324,4,1024]{2,0,1:T(8,128)(2,1)} all-to-all(bf16[324,4,1024]{2,0,1:T(8,128)(2,1)} %bitcast.124), channel_id=1, replica_groups=mesh['spec'=4,'space'=8] {'spec'}, dimensions={1} | all-to-all | bytes 5308416 | tf_op jit(solution)/shard_map/all_to_all | solution.py:168
  131.0 3.1 squeeze.16
  134.1 7.3 %fusion.39 = f32[1024,1296]{0,1:T(8,128)} fusion(bf16[1296,512]{1,0:T(8,128)(2,1)S(1)} %copy-done, bf16[1296,1024]{1,0:T(8,128)(2,1)} %squeeze.16, bf16[512,1296]{0,1:T(8,128)(2,1)S(1)} %copy-done.28), kind=kOutput, calls=%fused_computation.75 | convolution fusion | flops 2719481856 | bytes 10616832 | tf_op jit(solution)/shard_map/dot_general | solution.py:99
  141.3 5.8 fusion.33
  147.7 5.4 reduce.10
  153.1 4.2 reshape.260
  157.3 4.9 all-to-all-start.1
  164.9 5.6 fusion.96
  170.6 3.9 fusion.28
  174.7 53.9 %all_gather.7 = f32[2,4,1024]{2,0,1:T(2,128)S(1)} all-gather(f32[2,1,1024]{2,0,1:T(2,128)S(1)} %copy.71), channel_id=1, replica_groups=mesh['spec'=4,'space'=8] {'spec'}, dimensions={1}, use_global_device_ids=true | all-gather | bytes 40960 | tf_op jit(solution)/shard_map/all_gather | solution.py:160
  230.5 5.6 reshape.261
  236.1 57.6 %reduce.2 = bf16[1296,1024]{1,0:T(8,128)(2,1)} reduce(bf16[1296,1,1024]{2,1,0:T(2,128)(2,1)} %reshape.261, bf16[]{:T(256)} %constant.134), dimensions={1}, to_apply=%all_to_all.51.reduce_sub_computation | reduce | bytes 5308418 | tf_op jit(solution)/shard_map/all_to_all | solution.py:174
  293.7 3.1 all_to_all.52
  296.8 4.0 gather_fusion.2
  303.3 5.8 copy.63
  309.1 7.7 %reshape.199 = f32[324,16,256]{2,1,0:T(8,128)} reshape(f32[324,4,1024]{2,1,0:T(4,128)} %copy.63) | data formatting | bytes 10616832 | tf_op jit(solution)/shard_map/convert_element_type | solution.py:83
  316.8 3.4 add_multiply_fusion.1
  322.6 3.6 collective-permute-start.3
  326.3 6.9 %fusion.7 = f32[324,16,257]{2,1,0:T(8,128)S(1)} fusion(f32[324,16,256]{2,1,0:T(8,128)S(1)} %get-tuple-element.19, pred[324]{0:T(512)(128)(4,1)S(1)} %copy-done.25), kind=kLoop, calls=%fused_computation.21 | loop fusion | flops 14655168 | bytes 10637892 | tf_op jit(solution)/shard_map/jit(_where)/select_n | solution.py:76
  334.7 8.1 %fusion.12 = f32[324,17,256]{2,1,0:T(8,128)} fusion(f32[324,2,256]{2,1,0:T(2,128)S(1)} %collective-permute-done.3, f32[324,16,256]{2,1,0:T(8,128)S(1)} %get-tuple-element.18, f32[324,2,256]{2,1,0:T(2,128)S(1)} %collective-permute-done.2, pred[324]{0:T(512)(128)(4,1)S(1)} %copy-done.23), kind=kLoop, calls=%fused_computation.27 | loop fusion | flops 21150720 | bytes 12276036 | tf_op jit(solution)/shard_map/jit(_where)/select_n | solution.py:76
  342.8 7.7 %fusion.22 = bf16[324,16,256]{2,1,0:T(8,128)(2,1)} fusion(f32[324,16,257]{2,1,0:T(8,128)S(1)} %fusion.7, f32[324,17,256]{2,1,0:T(8,128)} %fusion.12, f32[324,16,256]{2,1,0:T(8,128)S(1)} %bitcast.118, f32[16,256]{1,0:T(8,128)S(1)} %copy-done.10), kind=kLoop, calls=%fused_computation.46 | loop fusion | flops 9289728 | bytes 29212672 | tf_op jit(solution)/shard_map/convert_element_type | solution.py:93
  350.5 6.1 %reshape.196 = bf16[324,4,1024]{2,1,0:T(4,128)(2,1)} reshape(bf16[324,16,256]{2,1,0:T(8,128)(2,1)} %fusion.22) | data formatting | bytes 5308416 | tf_op jit(solution)/shard_map/reshape | solution.py:165
  356.6 4.1 copy.72
  360.7 4.2 gather_fusion.4
  364.8 64.2 %all_to_all.67 = bf16[324,4,1024]{2,0,1:T(8,128)(2,1)} all-to-all(bf16[324,4,1024]{2,0,1:T(8,128)(2,1)} %bitcast.121), channel_id=1, replica_groups=mesh['spec'=4,'space'=8] {'spec'}, dimensions={1} | all-to-all | bytes 5308416 | tf_op jit(solution)/shard_map/all_to_all | solution.py:168
  432.1 7.3 %fusion.38 = f32[1024,1296]{0,1:T(8,128)} fusion(bf16[1296,512]{1,0:T(8,128)(2,1)S(1)} %copy-done, bf16[1296,1024]{1,0:T(8,128)(2,1)} %squeeze.19, bf16[512,1296]{0,1:T(8,128)(2,1)S(1)} %copy-done.29), kind=kOutput, calls=%fused_computation.74 | convolution fusion | flops 2719481856 | bytes 10616832 | tf_op jit(solution)/shard_map/dot_general | solution.py:99
  439.4 5.9 fusion.32
  445.3 5.3 reduce.11
  450.7 4.1 reshape.262
  454.8 4.8 all-to-all-start.3
  459.7 5.3 fusion.95
  465.0 6.5 %fusion.30 = f32[64,1024]{1,0:T(8,128)S(1)} fusion(f32[1024,1296]{0,1:T(8,128)} %fusion.38, bf16[1296,1024]{1,0:T(8,128)(2,1)S(1)} %copy-done.2, f32[32,1296]{1,0:T(8,128)S(1)} %get-tuple-element.41, f32[32,1296]{1,0:T(8,128)S(1)} %get-tuple-element.40), kind=kOutput, calls=%fused_computation.64 | convolution fusion | flops 1023363072 | bytes 8556544 | tf_op jit(solution)/shard_map/dot_general | solution.py:103
  472.7 45.7 %all-to-all-done.3 = bf16[4,2,165888]{2,1,0:T(2,128)(2,1)} async-done(((bf16[4,2,165888]{2,1,0:T(2,128)(2,1)}), bf16[4,2,165888]{2,1,0:T(2,128)(2,1)}, u32[]{:S(2)}, u32[]{:S(2)}) %all-to-all-start.3) | async-done | bytes 2654240 | tf_op jit(solution)/shard_map/all_to_all | solution.py:174
  518.4 5.6 reshape.263
  524.0 57.8 %reduce.5 = bf16[1296,1024]{1,0:T(8,128)(2,1)} reduce(bf16[1296,1,1024]{2,1,0:T(2,128)(2,1)} %reshape.263, bf16[]{:T(256)} %constant.134), dimensions={1}, to_apply=%all_to_all.58.reduce_sub_computation | reduce | bytes 5308418 | tf_op jit(solution)/shard_map/all_to_all | solution.py:174
  581.9 3.1 all_to_all.59
  585.0 4.1 gather_fusion.5
  589.1 5.4 copy.74
  594.5 5.9 reshape.197
  (129 shorter events, 24.6 us)
Async XLA Ops:
  0.6 133.4 %copy-start = (bf16[1296,512]{1,0:T(8,128)(2,1)S(1)}, bf16[1296,512]{1,0:T(8,128)(2,1)}, u32[]{:S(2)}) copy-start(bf16[1296,512]{1,0:T(8,128)(2,1)} %param.12) | copy-start | bytes 3981316
  2.3 294.5 %copy-start.20 = (s32[1024]{0:T(1024)}, s32[1024]{0:T(1024)S(1)}, u32[]{:S(2)}) copy-start(s32[1024]{0:T(1024)S(1)} %pad_clamp_fusion.1) | copy-start | bytes 12292
  3.0 43.6 %copy-start.9 = (f32[16,256]{1,0:T(8,128)}, f32[16,256]{1,0:T(8,128)S(1)}, u32[]{:S(2)}) copy-start(f32[16,256]{1,0:T(8,128)S(1)} %convert_element_type.117) | copy-start | bytes 49156
  18.4 2.7 copy-start.18
  18.4 2.7 copy-start.19
  18.4 8.7 %copy-start.30 = (s32[4]{0:T(128)S(1)}, s32[4]{0:T(128)}, u32[]{:S(2)}) copy-start(s32[4]{0:T(128)} %param.10) | copy-start | bytes 52
  21.5 12.7 %collective-permute-start = (f32[324,2,256]{2,1,0:T(2,128)S(1)}, f32[324,2,256]{2,1,0:T(2,128)S(1)}, u32[]{:S(2)}, u32[]{:S(2)}) collective-permute-start(f32[324,2,256]{2,1,0:T(2,128)S(1)} %get-tuple-element.22), channel_id=1, source_target_pairs={{0,1},{1,2},{2,3},{3,4},{4,5},{5,6},{6,7},{8,9},{9,10},{10,11},{11... | collective-permute-start | bytes 1990664 | tf_op jit(solution)/shard_map/ppermute | solution.py:31
  23.5 16.2 %collective-permute-start.1 = (f32[324,2,256]{2,1,0:T(2,128)S(1)}, f32[324,2,256]{2,1,0:T(2,128)S(1)}, u32[]{:S(2)}, u32[]{:S(2)}) collective-permute-start(f32[324,2,256]{2,1,0:T(2,128)S(1)} %get-tuple-element.23), channel_id=1, source_target_pairs={{1,0},{2,1},{3,2},{4,3},{5,4},{6,5},{7,6},{9,8},{10,9},{11,10},{12... | collective-permute-start | bytes 1990664 | tf_op jit(solution)/shard_map/ppermute | solution.py:33
  27.2 33.0 %copy-start.21 = (s32[1024]{0:T(1024)}, s32[1024]{0:T(1024)S(1)}, u32[]{:S(2)}) copy-start(s32[1024]{0:T(1024)S(1)} %pad_clamp_fusion) | copy-start | bytes 12292
  27.3 7.0 %copy-start.24 = (pred[324]{0:T(512)(128)(4,1)}, pred[324]{0:T(512)(128)(4,1)S(1)}, u32[]{:S(2)}) copy-start(pred[324]{0:T(512)(128)(4,1)S(1)} %get-tuple-element.47) | copy-start | bytes 976
  27.3 12.4 %copy-start.22 = (pred[324]{0:T(512)(128)(4,1)}, pred[324]{0:T(512)(128)(4,1)S(1)}, u32[]{:S(2)}) copy-start(pred[324]{0:T(512)(128)(4,1)S(1)} %get-tuple-element.46) | copy-start | bytes 976
  39.7 7.0 %copy-start.3 = (bf16[324,16,256]{2,1,0:T(8,128)(2,1)S(1)}, bf16[324,16,256]{2,1,0:T(8,128)(2,1)}, u32[]{:S(2)}) copy-start(bf16[324,16,256]{2,1,0:T(8,128)(2,1)} %param.8) | copy-start | bytes 7962628
  64.2 69.8 %copy-start.28 = (bf16[512,1296]{0,1:T(8,128)(2,1)S(1)}, bf16[512,1296]{0,1:T(8,128)(2,1)}, u32[]{:S(2)}) copy-start(bf16[512,1296]{0,1:T(8,128)(2,1)} %param.11) | copy-start | bytes 3981316
  153.1 10.7 %copy-start.5 = (f32[32,1,1,1024]{3,2,1,0:T(1,128)S(1)}, f32[32,1,1,1024]{3,2,1,0:T(1,128)}, u32[]{:S(2)}) copy-start(f32[32,1,1,1024]{3,2,1,0:T(1,128)} %param.14) | copy-start | bytes 393220
  153.1 10.7 %copy-start.13 = (s32[1,1,1024]{2,1,0:T(1,128)S(1)}, s32[1,1,1024]{2,1,0:T(1,128)}, u32[]{:S(2)}) copy-start(s32[1,1,1024]{2,1,0:T(1,128)} %param.15) | copy-start | bytes 12292
  153.1 11.0 %copy-start.4 = (f32[2,32,1,1,1024]{4,3,2,1,0:T(1,128)S(1)}, f32[2,32,1,1,1024]{4,3,2,1,0:T(1,128)}, u32[]{:S(2)}) copy-start(f32[2,32,1,1,1024]{4,3,2,1,0:T(1,128)} %param.13) | copy-start | bytes 786436
  157.3 13.2 %slice-start = ((s8[5308416]{0:T(1024)(128)(4,1)}), s8[1114112]{0:T(1024)(128)(4,1)S(1)}, s32[]{:S(2)}) async-start(s8[5308416]{0:T(1024)(128)(4,1)} %bitcast.115), calls=%async_computation.4 | async-start | bytes 2228224
  157.3 73.3 %all-to-all-start.1 = ((bf16[4,2,165888]{2,1,0:T(2,128)(2,1)}), bf16[4,2,165888]{2,1,0:T(2,128)(2,1)}, u32[]{:S(2)}, u32[]{:S(2)}) async-start(bf16[4,2,165888]{2,1,0:T(2,128)(2,1)} %reshape.260), calls=%async_computation.1 | async-start | bytes 5308416 | tf_op jit(solution)/shard_map/all_to_all | solution.py:174
  163.5 7.0 %copy-start.1 = (bf16[1296,1024]{1,0:T(8,128)(2,1)S(1)}, bf16[1296,1024]{1,0:T(8,128)(2,1)}, u32[]{:S(2)}) copy-start(bf16[1296,1024]{1,0:T(8,128)(2,1)} %squeeze.16) | copy-start | bytes 7962628
  163.8 0.7 copy-start.7
  163.8 10.7 %copy-start.26 = (f32[32]{0:T(128)}, f32[32]{0:T(128)S(1)}, u32[]{:S(2)}) copy-start(f32[32]{0:T(128)S(1)} %compare_convert_fusion) | copy-start | bytes 388
  164.1 10.4 %copy-start.14 = (f32[1,1296]{1,0:T(1,128)}, f32[1,1296]{1,0:T(1,128)S(1)}, u32[]{:S(2)}) copy-start(f32[1,1296]{1,0:T(1,128)S(1)} %get-tuple-element.54) | copy-start | bytes 15556
  164.1 10.4 %copy-start.16 = (f32[1,1296]{1,0:T(1,128)}, f32[1,1296]{1,0:T(1,128)S(1)}, u32[]{:S(2)}) copy-start(f32[1,1296]{1,0:T(1,128)S(1)} %get-tuple-element.55) | copy-start | bytes 15556
  164.1 0.6 copy-start.11
  164.2 6.4 %slice-start.1 = ((s8[5308416]{0:T(1024)(128)(4,1)}), s8[4194304]{0:T(1024)(128)(4,1)S(1)}, s32[]{:S(2)}) async-start(s8[5308416]{0:T(1024)(128)(4,1)} %bitcast.115), calls=%async_computation.5 | async-start | bytes 8388608
  316.8 9.5 %copy-start.25 = (pred[324]{0:T(512)(128)(4,1)S(1)}, pred[324]{0:T(512)(128)(4,1)}, u32[]{:S(2)}) copy-start(pred[324]{0:T(512)(128)(4,1)} %copy-done.24) | copy-start | bytes 976
  320.7 12.6 %collective-permute-start.2 = (f32[324,2,256]{2,1,0:T(2,128)S(1)}, f32[324,2,256]{2,1,0:T(2,128)S(1)}, u32[]{:S(2)}, u32[]{:S(2)}) collective-permute-start(f32[324,2,256]{2,1,0:T(2,128)S(1)} %get-tuple-element.20), channel_id=1, source_target_pairs={{0,1},{1,2},{2,3},{3,4},{4,5},{5,6},{6,7},{8,9},{9,10},{10,11},{11... | collective-permute-start | bytes 1990664 | tf_op jit(solution)/shard_map/ppermute | solution.py:31
  322.6 12.1 %collective-permute-start.3 = (f32[324,2,256]{2,1,0:T(2,128)S(1)}, f32[324,2,256]{2,1,0:T(2,128)S(1)}, u32[]{:S(2)}, u32[]{:S(2)}) collective-permute-start(f32[324,2,256]{2,1,0:T(2,128)S(1)} %get-tuple-element.21), channel_id=1, source_target_pairs={{1,0},{2,1},{3,2},{4,3},{5,4},{6,5},{7,6},{9,8},{10,9},{11,10},{12... | collective-permute-start | bytes 1990664 | tf_op jit(solution)/shard_map/ppermute | solution.py:33
  326.3 8.4 %copy-start.23 = (pred[324]{0:T(512)(128)(4,1)S(1)}, pred[324]{0:T(512)(128)(4,1)}, u32[]{:S(2)}) copy-start(pred[324]{0:T(512)(128)(4,1)} %copy-done.22) | copy-start | bytes 976
  326.3 16.6 %slice-start.2 = ((s8[5308416]{0:T(1024)(128)(4,1)}), s8[4194304]{0:T(1024)(128)(4,1)S(1)}, s32[]{:S(2)}) async-start(s8[5308416]{0:T(1024)(128)(4,1)} %bitcast.117), calls=%async_computation.6 | async-start | bytes 8388608
  333.2 9.6 %slice-start.3 = ((s8[5308416]{0:T(1024)(128)(4,1)}), s8[1114112]{0:T(1024)(128)(4,1)S(1)}, s32[]{:S(2)}) async-start(s8[5308416]{0:T(1024)(128)(4,1)} %bitcast.117), calls=%async_computation.7 | async-start | bytes 2228224
  333.2 9.6 %copy-start.10 = (f32[16,256]{1,0:T(8,128)S(1)}, f32[16,256]{1,0:T(8,128)}, u32[]{:S(2)}) copy-start(f32[16,256]{1,0:T(8,128)} %copy-done.9) | copy-start | bytes 49156
  364.8 67.3 %copy-start.29 = (bf16[512,1296]{0,1:T(8,128)(2,1)S(1)}, bf16[512,1296]{0,1:T(8,128)(2,1)}, u32[]{:S(2)}) copy-start(bf16[512,1296]{0,1:T(8,128)(2,1)} %param.11) | copy-start | bytes 3981316
  450.7 8.9 %copy-start.8 = (f32[31,1,1,1024]{3,2,1,0:T(1,128)S(1)}, f32[31,1,1,1024]{3,2,1,0:T(1,128)}, u32[]{:S(2)}) copy-start(f32[31,1,1,1024]{3,2,1,0:T(1,128)} %copy-done.7) | copy-start | bytes 380932
  450.7 8.9 %copy-start.12 = (pred[32,1024]{1,0:T(8,128)(4,1)S(1)}, pred[32,1024]{1,0:T(8,128)(4,1)}, u32[]{:S(2)}) copy-start(pred[32,1024]{1,0:T(8,128)(4,1)} %copy-done.11) | copy-start | bytes 98308
  450.7 9.0 %copy-start.15 = (f32[1,1296]{1,0:T(1,128)S(1)}, f32[1,1296]{1,0:T(1,128)}, u32[]{:S(2)}) copy-start(f32[1,1296]{1,0:T(1,128)} %copy-done.14) | copy-start | bytes 15556
  450.7 9.0 %copy-start.17 = (f32[1,1296]{1,0:T(1,128)S(1)}, f32[1,1296]{1,0:T(1,128)}, u32[]{:S(2)}) copy-start(f32[1,1296]{1,0:T(1,128)} %copy-done.16) | copy-start | bytes 15556
  454.8 63.6 %all-to-all-start.3 = ((bf16[4,2,165888]{2,1,0:T(2,128)(2,1)}), bf16[4,2,165888]{2,1,0:T(2,128)(2,1)}, u32[]{:S(2)}, u32[]{:S(2)}) async-start(bf16[4,2,165888]{2,1,0:T(2,128)(2,1)} %reshape.262), calls=%async_computation.3 | async-start | bytes 5308416 | tf_op jit(solution)/shard_map/all_to_all | solution.py:174
  459.6 5.4 copy-start.2
  465.0 6.5 %copy-start.6 = (f32[32,1,1,1024]{3,2,1,0:T(1,128)S(1)}, f32[32,1,1,1024]{3,2,1,0:T(1,128)}, u32[]{:S(2)}) copy-start(f32[32,1,1,1024]{3,2,1,0:T(1,128)} %param.14) | copy-start | bytes 393220
  465.0 6.5 %copy-start.27 = (f32[32]{0:T(128)S(1)}, f32[32]{0:T(128)}, u32[]{:S(2)}) copy-start(f32[32]{0:T(128)} %copy-done.26) | copy-start | bytes 388
where the time goes:
time: 608 us; the launch traced here: 601 us
  blocking collectives  198 us (33%)
  other arithmetic  191 us (31%)
  local copies, waits for them, and re-layouts  99.9 us (16%)
  waiting for transfers between devices  52.6 us (9%)
  matrix products  35.9 us (6%)
  starting transfers between devices  20.8 us (3%)
    all_to_all x2, blocking collectives, body(): lax.all_to_all(blocks, 'spec', split_axis=1, concat_axis=0, tiled=True)  131 us
    all_to_all x2, other arithmetic, body(): lax.all_to_all(updated[:, None, :], 'spec', split_axis=0, concat_axis=1,...  115 us
    all_gather x2, blocking collectives, body(): gathered = lax.all_gather(surface, 'spec', axis=1, tiled=True)  67.2 us
    all_to_all x2, waiting for transfers between devices, body(): lax.all_to_all(updated[:, None, :], 'spec', split_axis=0, concat_axis=1,...  45.7 us
    select_n x4, other arithmetic, face_difference(): face_flux = jnp.where(forward_mask, forward, backward)  29 us
    broadcast_in_dim x4, other arithmetic, body(): updated[:, None, :]  22.5 us
    unnamed x76, local copies, waits for them, and re-layouts  21.9 us
    reshape x4, local copies, waits for them, and re-layouts, body(): blocks = drifted.reshape(local_comps, slot_count, block_points)  20.4 us
  transfers between devices with their start and end apart: 6, of which 3 were waited for; matrix products, arithmetic and copies ran while one was open for 7% of the time, Pallas kernels for 0%

commit v1 on v0

v1 whole, which is shorter than its diff:
```python
import functools
import math

import jax
import jax.numpy as jnp
from jax import lax
from jax.experimental import pallas as pl
from jax.experimental.pallas import tpu as pltpu
from jax.sharding import PartitionSpec as P

NDIR = 36
NFREQ = 36
K = NDIR * NFREQ
STEPS = 2

courant_scale = 0.5
current_scale = 0.15
source_step = 0.25
coriolis = 0.3
stress_scale = 0.5
drift_scale = 4.0

MESH = pl.DeviceIdType.MESH
F32 = jnp.float32
BF16 = jnp.bfloat16
VMEM_LIMIT = 60 * 1024 * 1024
ROWS = 16


def tap_tables(first, count, padded):
    component = jnp.minimum(first + jnp.arange(padded, dtype=jnp.int32), K - 1)
    frequency = component // NDIR
    direction = component % NDIR
    angle = (direction.astype(F32) + 0.5) * (2.0 * math.pi / NDIR)
    speed = courant_scale * jnp.exp(-2.0 * frequency.astype(F32) / NFREQ)
    eastward = (4 * direction + 2 < NDIR) | (4 * direction + 2 > 3 * NDIR)
    northward = 2 * direction + 1 < NDIR
    forward = (1.0 / 6.0, -1.0, 0.5, 2.0 / 6.0, 0.0)
    backward = (0.0, -2.0 / 6.0, -0.5, 1.0, -1.0 / 6.0)
    columns = [speed * jnp.cos(angle), speed * jnp.sin(angle)]
    for mask in (eastward, northward):
        for f, b in zip(forward, backward):
            columns.append(jnp.where(mask, F32(f), F32(b)))
    return jnp.stack(columns, 1)


def coupling_tables(layers):
    component = jnp.arange(K, dtype=jnp.int32)
    frequency = (component // NDIR).astype(F32)
    direction = (component % NDIR).astype(F32)
    angle = (direction + 0.5) * (2.0 * math.pi / NDIR)
    wavenum = 0.02 * jnp.exp(6.0 * frequency / NFREQ)
    depth = jnp.arange(layers, dtype=F32)[:, None] + 0.5
    decay_rows = wavenum[None, :] ** 1.5 * jnp.exp(-2.0 * wavenum[None, :] * depth)
    decay_rows = decay_rows / jnp.sqrt(jnp.sum(decay_rows * decay_rows, axis=1, keepdims=True))
    drift_rows = drift_scale * jnp.concatenate(
        [decay_rows * jnp.cos(angle)[None, :], decay_rows * jnp.sin(angle)[None, :]], 0
    )
    stress = wavenum / jnp.sqrt(jnp.sum(wavenum * wavenum))
    stress_rows = -stress_scale * jnp.stack([stress * jnp.cos(angle), stress * jnp.sin(angle)], 0)
    return (drift_rows, stress_rows)


def pieces(rows):
    first = lax.reduce_precision(rows, 8, 7)
    rest = rows - first
    second = lax.reduce_precision(rest, 8, 7)
    third = rest - second
    return jnp.concatenate([first, second, third], 0).astype(BF16)


def advect_kernel(width, owners, state, before, after, land, east, north, taps, rank, out, drift):
    slots, chunks, comps, chunk_width = out.shape
    padded, points = state.shape
    rows = points // width
    block = points // slots
    column = lax.broadcasted_iota(jnp.int32, (ROWS, width), 1)

    def shifted(value, by):
        turned = pltpu.roll(value, by % width, 1)
        inside = (column >= by) if by > 0 else (column < width + by)
        return jnp.where(inside, turned, 0.0)

    def chunk(index, carry):
        here = pl.ds(pl.multiple_of(index * ROWS, ROWS), ROWS)
        tap = taps[here, :]

        def spread(i):
            return jnp.broadcast_to(tap[:, i : i + 1], (ROWS, width))

        speed_east, speed_north = spread(0), spread(1)
        row_tap = [spread(2 + i) for i in range(5)]
        col_tap = [spread(7 + i) for i in range(5)]

        def masked_row(r):
            if r < 0:
                return before[here, (r + 2) * width : (r + 3) * width].astype(F32)
            if r >= rows:
                return after[here, (r - rows) * width : (r - rows + 1) * width].astype(F32)
            at = slice(r * width, (r + 1) * width)
            return state[here, at].astype(F32) * land[:, at]

        def flux(r, masked):
            at = slice((r + 2) * width, (r + 3) * width)
            return (speed_east + current_scale * east[:, at]) * masked

        masked = {}
        flow = {}
        for r in range(-2, rows + 2):
            masked[r] = masked_row(r)
            flow[r] = flux(r, masked[r])
            c = r - 2
            if c < 0:
                continue
            at = slice(c * width, (c + 1) * width)
            m = masked.pop(c)
            along = (speed_north + current_scale * north[:, at]) * m
            total = m
            for i in range(5):
                total = total - row_tap[i] * flow[c - 2 + i]
            total = total - col_tap[2] * along
            for i in (0, 1, 3, 4):
                total = total - col_tap[i] * shifted(along, 2 - i)
            flow.pop(c - 2)
            b, inner = c * width // block, c * width % block
            drift[b, here, inner : inner + width] = (total * land[:, at]).astype(BF16)
        return carry

    lax.fori_loop(0, padded // ROWS, chunk, 0)

    position = lax.broadcasted_iota(jnp.int32, (chunks * chunk_width, block), 0)

    def pack(s, carry):
        b = owners[s]
        spot = (position == rank[b]).astype(F32).astype(BF16)
        packed = lax.dot_general(
            drift[b], spot, (((1,), (1,)), ((), ())), preferred_element_type=F32
        ).astype(BF16)
        for j in range(chunks):
            out[s, j] = packed[:comps, j * chunk_width : (j + 1) * chunk_width]
        return carry

    lax.fori_loop(0, slots, pack, 0)


def expand_kernel(inverse, packed, rank, out):
    chunks, slots, comps, chunk_width = packed.shape
    padded, block = out.shape[1:]
    position = lax.broadcasted_iota(jnp.int32, (chunk_width, block), 0)

    def expand(b, carry):
        s = inverse[b]
        total = jnp.zeros((comps, block), F32)
        for j in range(chunks):
            spot = (position + j * chunk_width == rank[b]).astype(F32).astype(BF16)
            total = total + jnp.dot(packed[j, s], spot, preferred_element_type=F32)
        out[b, :comps, :] = total.astype(BF16)
        if padded > comps:
            out[b, comps:, :] = jnp.zeros((padded - comps, block), BF16)
        return carry

    lax.fori_loop(0, slots, expand, 0)


def source_kernel(
    layers, blocks, proj, back, inner, velocity, mixing, active, rank,
    returned, new_velocity, surfaces,
    got, made, pay, surface,
    send_in, recv_in, send_back, recv_back, send_top, recv_top,
):
    slots, chunks, comps, chunk_width = blocks.shape
    rank_rows = back.shape[2]
    points = rank.shape[1]
    me = lax.axis_index("spec")

    def peer(delta):
        return lax.rem(me + delta, slots)

    barrier = pltpu.get_barrier_semaphore()
    for delta in range(1, slots):
        pl.semaphore_signal(
            barrier, inc=1, device_id={"spec": peer(delta)}, device_id_type=MESH
        )
    pl.semaphore_wait(barrier, slots - 1)

    def inward(j, delta):
        return pltpu.make_async_remote_copy(
            src_ref=blocks.at[peer(delta), j],
            dst_ref=got.at[j, me],
            send_sem=send_in.at[j, delta],
            recv_sem=recv_in.at[j, delta],
            device_id={"spec": peer(delta)},
            device_id_type=MESH,
        )

    def homeward(j, delta):
        return pltpu.make_async_remote_copy(
            src_ref=made.at[j, peer(delta)],
            dst_ref=returned.at[j, me],
            send_sem=send_back.at[j, delta],
            recv_sem=recv_back.at[j, delta],
            device_id={"spec": peer(delta)},
            device_id_type=MESH,
        )

    for j in range(chunks):
        for delta in range(1, slots):
            inward(j, delta).start()
    for j in range(chunks):
        got[j, me] = blocks[me, j]

    def one_chunk(j, carry):
        for delta in range(1, slots):
            inward(j, delta).wait_recv()
        full = jnp.dot(proj[0], got[j, 0], preferred_element_type=F32)
        for g in range(1, slots):
            full = full + jnp.dot(proj[g], got[j, g], preferred_element_type=F32)
        projected = full[:rank_rows]
        cubed = (projected * projected * projected).astype(BF16)
        for delta in list(range(1, slots)) + [0]:
            g = peer(delta)
            transfer = jnp.dot(back[g], cubed, preferred_element_type=F32)
            updated = (got[j, g].astype(F32) + source_step * transfer).astype(BF16)
            made[j, g] = updated
            if delta:
                homeward(j, delta).start()
            else:
                returned[j, g] = updated
        drift = full[rank_rows:]
        third = drift.shape[0] // 3
        drift = drift[:third] + drift[third : 2 * third] + drift[2 * third :]
        more = jnp.dot(inner[...], cubed, preferred_element_type=F32)
        third = more.shape[0] // 3
        pay[j] = drift + (more[:third] + more[third : 2 * third] + more[2 * third :])
        return carry

    lax.fori_loop(0, chunks, one_chunk, 0)

    position = lax.broadcasted_iota(jnp.int32, (chunk_width, points), 0)
    payload = None
    for j in range(chunks):
        spot = (position + j * chunk_width == rank[...]).astype(F32).astype(BF16)
        value = pay[j]
        for _ in range(3):
            part = value.astype(BF16)
            value = value - part.astype(F32)
            term = jnp.dot(part, spot, preferred_element_type=F32)
            payload = term if payload is None else payload + term

    layer = lax.broadcasted_iota(jnp.int32, (layers, points), 0)
    depth = active[...]
    live = (layer < depth).astype(F32)
    bottom = (layer == depth - 1).astype(F32)
    top = (layer == 0).astype(F32)
    mix = mixing[...]
    upper = mix * ((layer + 1 < depth) & (layer < layers - 1)).astype(F32)

    def mixed(field):
        between = upper * (field - pltpu.roll(field, layers - 1, 0))
        return pltpu.roll(between, 1, 0) - between - mix * bottom * field

    east, north = velocity[0], velocity[1]
    drift_east = payload[:layers]
    drift_north = payload[layers : 2 * layers]
    stress_east = payload[2 * layers : 2 * layers + 1]
    stress_north = payload[2 * layers + 1 : 2 * layers + 2]
    new_east = live * (east + coriolis * (north + drift_north) + mixed(east) + top * stress_east)
    new_north = live * (north - coriolis * (east + drift_east) + mixed(north) + top * stress_north)
    new_velocity[0] = new_east
    new_velocity[1] = new_north
    surface[0:1, :] = new_east[0:1]
    surface[1:2, :] = new_north[0:1]
    surfaces[me] = surface[...]

    def upward(delta):
        return pltpu.make_async_remote_copy(
            src_ref=surface,
            dst_ref=surfaces.at[me],
            send_sem=send_top.at[delta],
            recv_sem=recv_top.at[delta],
            device_id={"spec": peer(delta)},
            device_id_type=MESH,
        )

    for delta in range(1, slots):
        upward(delta).start()
    for delta in range(1, slots):
        upward(delta).wait()
    for j in range(chunks):
        for delta in range(1, slots):
            inward(j, delta).wait_send()
            homeward(j, delta).wait()


def whole(count, memory=pltpu.VMEM):
    return [pl.BlockSpec(memory_space=memory)] * count


def shift_rows(head, tail):
    count = lax.axis_size("space")
    up = [(i, i + 1) for i in range(count - 1)]
    down = [(i + 1, i) for i in range(count - 1)]
    return lax.ppermute(tail, "space", up), lax.ppermute(head, "space", down)


def body(spectrum, land_sea, owners, proj_weight, back_weight, ocean_vel, mixing, active_layers):
    comps, rows, width = spectrum.shape
    slots = lax.axis_size("spec")
    points = rows * width
    block = points // slots
    cap = block * 3 // 4
    chunk_width = 256 if cap % 256 == 0 else cap
    chunks = cap // chunk_width
    layers = mixing.shape[0]
    rank_rows = proj_weight.shape[0]
    padded = -(-comps // ROWS) * ROWS
    me = lax.axis_index("spec")

    inverse = jnp.sum(
        jnp.where(owners[:, None] == jnp.arange(slots)[None], jnp.arange(slots)[:, None], 0), 0
    ).astype(jnp.int32)
    taps = tap_tables(me * comps, comps, padded)
    drift_rows, stress_rows = coupling_tables(layers)
    zeros = jnp.zeros((6, K), F32)
    outer_rows = pieces(jnp.concatenate([drift_rows, zeros, zeros[:2]], 0))
    through = jnp.dot(
        jnp.concatenate([source_step * drift_rows, stress_rows, zeros], 0),
        back_weight.astype(F32),
        precision=lax.Precision.HIGHEST,
    )
    inner = pieces(through)
    proj = jnp.concatenate([proj_weight, outer_rows], 0)
    proj = jnp.transpose(proj.reshape(proj.shape[0], slots, comps), (1, 0, 2))
    back = back_weight.reshape(slots, comps, rank_rows)

    land = land_sea.astype(F32).reshape(1, points)
    sea = land_sea.reshape(slots, block)
    rank = jnp.where(sea > 0, jnp.cumsum(sea, 1) - 1, -1).reshape(slots, 1, block)
    my_rank = lax.dynamic_index_in_dim(rank, owners[me], 0, False)

    velocity = ocean_vel.reshape(2, layers, block)
    mixing_local = mixing.reshape(layers, block)
    active = active_layers.reshape(1, block)
    surfaces = lax.all_gather(velocity[:, 0], "spec", axis=0)
    head = (spectrum[:, :2] * land_sea[None, :2].astype(BF16)).reshape(comps, 2 * width)
    tail = (spectrum[:, -2:] * land_sea[None, -2:].astype(BF16)).reshape(comps, 2 * width)
    state = jnp.pad(spectrum.reshape(comps, points), ((0, padded - comps), (0, 0)))
    for _ in range(STEPS):
        before, after = shift_rows(head, tail)
        before = jnp.pad(before, ((0, padded - comps), (0, 0)))
        after = jnp.pad(after, ((0, padded - comps), (0, 0)))
        currents = sum(
            jnp.where((owners[s] == jnp.arange(slots))[:, None, None], surfaces[s][None], 0.0)
            for s in range(slots)
        )
        east = currents[:, 0].reshape(1, points)
        north = currents[:, 1].reshape(1, points)
        east_before, east_after = shift_rows(east[:, : 2 * width], east[:, -2 * width :])
        east = jnp.concatenate([east_before, east, east_after], 1)
        blocks = pl.pallas_call(
            functools.partial(advect_kernel, width),
            out_shape=jax.ShapeDtypeStruct((slots, chunks, comps, chunk_width), BF16),
            in_specs=whole(1, pltpu.SMEM) + whole(8),
            out_specs=pl.BlockSpec(memory_space=pltpu.VMEM),
            scratch_shapes=[pltpu.VMEM((slots, padded, block), BF16)],
            compiler_params=pltpu.CompilerParams(vmem_limit_bytes=VMEM_LIMIT),
            name="advect",
        )(owners, state, before, after, land, east, north, taps, rank)
        returned, velocity, surfaces = pl.pallas_call(
            functools.partial(source_kernel, layers),
            out_shape=(
                jax.ShapeDtypeStruct((chunks, slots, comps, chunk_width), BF16),
                jax.ShapeDtypeStruct((2, layers, block), F32),
                jax.ShapeDtypeStruct((slots, 2, block), F32),
            ),
            in_specs=whole(8),
            out_specs=tuple(whole(3)),
            scratch_shapes=[
                pltpu.VMEM((chunks, slots, comps, chunk_width), BF16),
                pltpu.VMEM((chunks, slots, comps, chunk_width), BF16),
                pltpu.VMEM((chunks, inner.shape[0] // 3, chunk_width), F32),
                pltpu.VMEM((2, block), F32),
                pltpu.SemaphoreType.DMA((chunks, slots)),
                pltpu.SemaphoreType.DMA((chunks, slots)),
                pltpu.SemaphoreType.DMA((chunks, slots)),
                pltpu.SemaphoreType.DMA((chunks, slots)),
                pltpu.SemaphoreType.DMA((slots,)),
                pltpu.SemaphoreType.DMA((slots,)),
            ],
            compiler_params=pltpu.CompilerParams(
                vmem_limit_bytes=VMEM_LIMIT, collective_id=0, has_side_effects=True
            ),
            name="source",
        )(blocks, proj, back, inner, velocity, mixing_local, active, my_rank)
        grid = pl.pallas_call(
            expand_kernel,
            out_shape=jax.ShapeDtypeStruct((slots, padded, block), BF16),
            in_specs=whole(1, pltpu.SMEM) + whole(2),
            out_specs=pl.BlockSpec(memory_space=pltpu.VMEM),
            compiler_params=pltpu.CompilerParams(vmem_limit_bytes=VMEM_LIMIT),
            name="expand",
        )(inverse, returned, rank)
        state = jnp.transpose(grid, (1, 0, 2)).reshape(padded, points)
        head = state[:comps, : 2 * width]
        tail = state[:comps, -2 * width :]
    return (state[:comps].reshape(comps, rows, width), velocity.reshape(ocean_vel.shape))


def solution(mesh):
    placed = (
        P("spec", "space", None),
        P("space", None),
        P(),
        P(),
        P(),
        P(None, None, "spec", "space", None),
        P(None, "spec", "space", None),
        P("spec", "space", None),
    )
    return jax.shard_map(
        body,
        mesh=mesh,
        in_specs=placed,
        out_specs=(P("spec", "space", None), P(None, None, "spec", "space", None)),
        check_vma=False,
    )
```

time: 608 us -> 336 us (0.55)
  Pallas kernels: 0 us -> 235 us
  blocking collectives: 198 us -> 13.4 us
  other arithmetic: 191 us -> 23.1 us
  local copies, waits for them, and re-layouts: 99.9 us -> 33.9 us
  waiting for transfers between devices: 52.6 us -> 3.48 us
  matrix products: 35.9 us -> 1.51 us
    pallas_call x0 -> x6, Pallas kernels: none -> 235 us  [the longest x2 192 us: body(): pl.pallas_call(functools.partial(source_kernel, layers), out_shape=(jax.S...]
    all_to_all x2 -> x0, blocking collectives: 131 us -> none  [body(): lax.all_to_all(blocks, 'spec', split_axis=1, concat_axis=0, tiled=True)]
    all_to_all x2 -> x0, other arithmetic: 115 us -> none  [body(): lax.all_to_all(updated[:, None, :], 'spec', split_axis=0, concat_axis=1,...]
    all_gather x2 -> x1, blocking collectives: 67.2 us -> 13.4 us  [body(): surfaces = lax.all_gather(velocity[:, 0], 'spec', axis=0)]
    all_to_all x2 -> x0, waiting for transfers between devices: 45.7 us -> none  [body(): lax.all_to_all(updated[:, None, :], 'spec', split_axis=0, concat_axis=1,...]
    dot_general x6 -> x1, matrix products: 35.9 us -> 1.51 us  [body(): jnp.dot(jnp.concatenate([source_step * drift_rows, stress_rows, zeros], 0...]
    select_n x7, other arithmetic: 29 us -> 4.44 us  [the longest x5 2.48 us: tap_tables(): columns.append(jnp.where(mask, F32(f), F32(b)))]
    gather x7 -> x0, local copies, waits for them, and re-layouts: 22.9 us -> none  [the longest x3 13.5 us: body(): returned = returned[:, inverse]]
  transfers between devices with their start and end apart: 6 -> 8, of which waited for: 3 -> 2; matrix products, arithmetic and copies ran while one was open for 7% -> 12% of each run, Pallas kernels for 0% -> 0%
where the time goes in v1:
time: 336 us; the launch traced here: 334 us
  Pallas kernels  235 us (70%)
  local copies, waits for them, and re-layouts  33.9 us (10%)
  other arithmetic  23.1 us (7%)
  starting transfers between devices  20.6 us (6%)
  blocking collectives  13.4 us (4%)
  between operations  3.69 us (1%)
  waiting for transfers between devices  3.48 us (1%)
    pallas_call x2, Pallas kernels, body(): pl.pallas_call(functools.partial(source_kernel, layers), out_shape=(jax.S...  192 us
    pallas_call x2, Pallas kernels, body(): pl.pallas_call(functools.partial(advect_kernel, width), out_shape=jax.Sha...  30.4 us
    ppermute x8, starting transfers between devices, shift_rows(): return (lax.ppermute(tail, 'space', up), lax.ppermute(head, 'space', down))  20.6 us
    all_gather x1, blocking collectives, body(): surfaces = lax.all_gather(velocity[:, 0], 'spec', axis=0)  13.4 us
    pallas_call x2, Pallas kernels, body(): pl.pallas_call(expand_kernel, out_shape=jax.ShapeDtypeStruct((slots, padd...  11.9 us
    unnamed x77, local copies, waits for them, and re-layouts  8.57 us
  transfers between devices with their start and end apart: 8, of which 2 were waited for; matrix products, arithmetic and copies ran while one was open for 12% of the time, Pallas kernels for 0%

profile of v1, /device:TPU:2, one launch (start us, length us, event | category | flops | bytes accessed | tf_op | source)
XLA Modules:
  0.0 334.3 jit_solution(17753798161734188138)
XLA Ops:
  0.7 1.4 convert_bitcast_fusion
  2.1 2.5 slice_multiply_fusion
  4.8 0.8 copy.51
  5.6 1.9 collective-permute-start
  7.8 0.8 copy.52
  8.6 3.8 %collective-permute-start.1 = (bf16[324,512]{1,0:T(8,128)(2,1)}, bf16[324,512]{1,0:T(8,128)(2,1)}, u32[]{:S(2)}, u32[]{:S(2)}) collective-permute-start(bf16[324,512]{1,0:T(8,128)(2,1)} %bitcast.31), channel_id=1, source_target_pairs={{1,0},{2,1},{3,2},{4,3},{5,4},{6,5},{7,6},{9,8},{10,9},{11,10},{12... | collective-permute-start | bytes 995336 | tf_op jit(solution)/shard_map/ppermute | solution.py:303
  12.5 13.4 %all-gather = f32[8,1,1024]{2,1,0:T(1,128)S(1)} all-gather(f32[2,1,1024]{2,1,0:T(1,128)S(1)} %slice.137), channel_id=2, replica_groups=mesh['spec'=4,'space'=8] {'spec'}, dimensions={0}, use_global_device_ids=true | all-gather | bytes 40960 | tf_op jit(solution)/shard_map/all_gather | solution.py:344
  25.9 0.7 fusion.43
  26.5 1.3 iota_compare_fusion.1
  27.8 1.2 iota_compare_fusion.3
  30.4 1.9 collective-permute-start.3
  32.3 2.4 collective-permute-start.2
  40.9 1.1 reduce-window.6
  42.4 0.7 add_add_fusion
  43.1 0.7 fusion.45
  46.1 0.7 copy.68
  46.8 1.4 broadcast_select_fusion.rank
  48.2 1.5 reduce-precision_convert_fusion.3
  50.3 1.7 pad_maximum_fusion.1.inner
  52.6 3.1 pad_maximum_fusion
  55.9 2.3 reshape.377.back
  58.2 1.2 copy.50
  59.6 1.8 pad.17.state
  62.7 0.8 copy.34.taps
  63.5 1.8 reshape.376
  65.3 2.5 copy.38
  68.4 1.3 pad_maximum_fusion.2.east
  69.7 0.8 pad.18.before
  70.5 1.8 pad.19.after
  72.2 15.2 %advect.2.blocks = bf16[4,3,324,256]{3,2,1,0:T(8,128)(2,1)} custom-call(s32[4]{0:T(128)} %owners.3, bf16[336,4096]{1,0:T(8,128)(2,1)} %pad.17.state, bf16[336,512]{1,0:T(8,128)(2,1)} %pad.18.before, bf16[336,512]{1,0:T(8,128)(2,1)} %pad.19.after, f32[1,4096]{1,0:T(1,128)} %bitcast.88, f32[1,5120]{1,0:T(1,128)} %pad_maximum_fusion.2.east, ...), custom_call_target="tpu_custom_call" | custom-call | tf_op jit(solution)/shard_map/advect/pallas_call | solution.py:360
  87.4 97.2 %source.2 = (bf16[3,4,324,256]{3,2,1,0:T(8,128)(2,1)}, f32[2,32,1024]{2,1,0:T(8,128)}, f32[4,2,1024]{2,1,0:T(2,128)}) custom-call(bf16[4,3,324,256]{3,2,1,0:T(8,128)(2,1)} %advect.2.blocks, bf16[4,728,324]{2,1,0:T(8,128)(2,1)} %bitcast.73, bf16[4,324,512]{2,1,0:T(8,128)(2,1)} %reshape.377.back, bf16[216,512]{1,0:T(8,128)(2,1)} %pad_maximum_fusion.1.inner, ...), custom_call_target="tpu_custom_call" | custom-call | tf_op jit(solution)/shard_map/source/pallas_call | solution.py:369
  184.6 6.0 %expand.2 = bf16[4,336,1024]{2,1,0:T(8,128)(2,1)} custom-call(s32[4]{0:T(128)} %select_reduce_fusion.inverse, bf16[3,4,324,256]{3,2,1,0:T(8,128)(2,1)} %get-tuple-element.7.packed, s32[4,1,1024]{2,1,0:T(1,128)} %broadcast_select_fusion.rank), custom_call_target="tpu_custom_call" | custom-call | tf_op jit(solution)/shard_map/expand/pallas_call | solution.py:395
  190.6 2.1 copy.49
  193.0 1.9 collective-permute-start.7
  194.9 2.4 collective-permute-start.6
  197.4 4.2 %collective-permute-start.4 = (bf16[324,512]{1,0:T(8,128)(2,1)S(1)}, bf16[324,512]{1,0:T(8,128)(2,1)S(1)}, u32[]{:S(2)}, u32[]{:S(2)}) collective-permute-start(bf16[324,512]{1,0:T(8,128)(2,1)S(1)} %get-tuple-element.23), channel_id=1, source_target_pairs={{0,1},{1,2},{2,3},{3,4},{4,5},{5,6},{6,7},{8,9},{9,10},{10,11},{11... | collective-permute-start | bytes 995336 | tf_op jit(solution)/shard_map/ppermute | solution.py:303
  201.5 2.1 collective-permute-start.5
  204.9 1.0 collective-permute-done.4
  205.9 0.8 pad.20.before
  206.6 2.5 collective-permute-done.5
  209.1 0.8 pad.21.after
  209.9 15.2 %advect.3.blocks = bf16[4,3,324,256]{3,2,1,0:T(8,128)(2,1)} custom-call(s32[4]{0:T(128)} %owners.3, bf16[336,4096]{1,0:T(8,128)(2,1)} %bitcast.76, bf16[336,512]{1,0:T(8,128)(2,1)} %pad.20.before, bf16[336,512]{1,0:T(8,128)(2,1)} %pad.21.after, f32[1,4096]{1,0:T(1,128)} %bitcast.89, f32[1,5120]{1,0:T(1,128)} %pad_maximum_fusion.3.east, f32[1,4096]{1,0:T(1,128)} %bitcast.95, ...), custom_call_target="tpu_custom_call" | custom-call | tf_op jit(solution)/shard_map/advect/pallas_call | solution.py:360
  225.1 95.3 %source.3 = (bf16[3,4,324,256]{3,2,1,0:T(8,128)(2,1)}, f32[2,32,1024]{2,1,0:T(8,128)}, f32[4,2,1024]{2,1,0:T(2,128)}) custom-call(bf16[4,3,324,256]{3,2,1,0:T(8,128)(2,1)} %advect.3.blocks, bf16[4,728,324]{2,1,0:T(8,128)(2,1)} %bitcast.74, bf16[4,324,512]{2,1,0:T(8,128)(2,1)} %reshape.377.back, bf16[216,512]{1,0:T(8,128)(2,1)} %pad_maximum_fusion.1.inner, ...), custom_call_target="tpu_custom_call" | custom-call | tf_op jit(solution)/shard_map/source/pallas_call | solution.py:369
  320.4 5.9 %expand.3 = bf16[4,336,1024]{2,1,0:T(8,128)(2,1)} custom-call(s32[4]{0:T(128)} %select_reduce_fusion.inverse, bf16[3,4,324,256]{3,2,1,0:T(8,128)(2,1)} %get-tuple-element.10.packed, s32[4,1,1024]{2,1,0:T(1,128)} %broadcast_select_fusion.rank), custom_call_target="tpu_custom_call" | custom-call | tf_op jit(solution)/shard_map/expand/pallas_call | solution.py:395
  326.3 2.0 slice.153
  328.3 2.0 copy.41
  330.4 3.0 reshape.381
  333.4 1.0 copy.42
  (120 shorter events, 13.2 us)
Async XLA Ops:
  0.6 37.7 %copy-start.6 = (s32[16,256]{1,0:T(8,128)S(1)}, s32[16,256]{1,0:T(8,128)}, u32[]{:S(2)}) copy-start(s32[16,256]{1,0:T(8,128)} %param.9) | copy-start | bytes 49156
  0.6 11.7 %copy-start.4 = (f32[2,32,1,1,1024]{4,3,2,1,0:T(1,128)S(1)}, f32[2,32,1,1,1024]{4,3,2,1,0:T(1,128)}, u32[]{:S(2)}) copy-start(f32[2,32,1,1,1024]{4,3,2,1,0:T(1,128)} %param.13) | copy-start | bytes 786436
  0.6 25.2 %copy-start.11 = (s32[4]{0:T(128)S(1)}, s32[4]{0:T(128)}, u32[]{:S(2)}) copy-start(s32[4]{0:T(128)} %owners.3) | copy-start | bytes 52
  5.6 64.1 %collective-permute-start = (bf16[324,512]{1,0:T(8,128)(2,1)}, bf16[324,512]{1,0:T(8,128)(2,1)S(1)}, u32[]{:S(2)}, u32[]{:S(2)}) collective-permute-start(bf16[324,512]{1,0:T(8,128)(2,1)} %bitcast.28), channel_id=1, source_target_pairs={{0,1},{1,2},{2,3},{3,4},{4,5},{5,6},{6,7},{8,9},{9,10},{10,11},{11... | collective-permute-start | bytes 995336 | tf_op jit(solution)/shard_map/ppermute | solution.py:303
  8.6 39.6 %copy-start.1 = (bf16[1296,512]{1,0:T(8,128)(2,1)S(1)}, bf16[1296,512]{1,0:T(8,128)(2,1)}, u32[]{:S(2)}) copy-start(bf16[1296,512]{1,0:T(8,128)(2,1)} %param.12) | copy-start | bytes 3981316
  8.6 61.9 %collective-permute-start.1 = (bf16[324,512]{1,0:T(8,128)(2,1)}, bf16[324,512]{1,0:T(8,128)(2,1)}, u32[]{:S(2)}, u32[]{:S(2)}) collective-permute-start(bf16[324,512]{1,0:T(8,128)(2,1)} %bitcast.31), channel_id=1, source_target_pairs={{1,0},{2,1},{3,2},{4,3},{5,4},{6,5},{7,6},{9,8},{10,9},{11,10},{12... | collective-permute-start | bytes 995336 | tf_op jit(solution)/shard_map/ppermute | solution.py:303
  12.4 37.2 %copy-start.3 = (f32[2,32,1,1,1024]{4,1,2,3,0:T(8,128)}, f32[2,32,1,1,1024]{4,1,2,3,0:T(8,128)S(1)}, u32[]{:S(2)}) copy-start(f32[2,32,1,1,1024]{4,1,2,3,0:T(8,128)S(1)} %copy.66) | copy-start | bytes 786436
  27.8 1.9 copy-start.21
  27.8 1.9 copy-start.23
  29.0 0.7 copy-start.25
  29.0 0.7 copy-start.27
  30.4 38.0 %collective-permute-start.3 = (f32[1,512]{1,0:T(1,128)}, f32[1,512]{1,0:T(1,128)}, u32[]{:S(2)}, u32[]{:S(2)}) collective-permute-start(f32[1,512]{1,0:T(1,128)} %get-tuple-element.49), channel_id=1, source_target_pairs={{1,0},{2,1},{3,2},{4,3},{5,4},{6,5},{7,6},{9,8},{10,9},{11,10},{12... | collective-permute-start | bytes 6152 | tf_op jit(solution)/shard_map/ppermute | solution.py:303
  32.3 36.1 %collective-permute-start.2 = (f32[1,512]{1,0:T(1,128)}, f32[1,512]{1,0:T(1,128)}, u32[]{:S(2)}, u32[]{:S(2)}) collective-permute-start(f32[1,512]{1,0:T(1,128)} %get-tuple-element.48), channel_id=1, source_target_pairs={{0,1},{1,2},{2,3},{3,4},{4,5},{5,6},{6,7},{8,9},{9,10},{10,11},{11... | collective-permute-start | bytes 6152 | tf_op jit(solution)/shard_map/ppermute | solution.py:303
  50.3 5.5 %copy-start.2 = (bf16[324,16,256]{2,1,0:T(8,128)(2,1)S(1)}, bf16[324,16,256]{2,1,0:T(8,128)(2,1)}, u32[]{:S(2)}) copy-start(bf16[324,16,256]{2,1,0:T(8,128)(2,1)} %param.8) | copy-start | bytes 7962628
  59.4 1.9 copy-start.8
  59.5 2.5 copy-start.9
  59.5 3.1 copy-start.12
  59.5 3.1 copy-start.13
  59.5 3.1 copy-start.14
  59.5 3.1 copy-start.15
  59.5 3.1 copy-start.16
  59.5 3.1 copy-start.17
  59.5 3.1 copy-start.18
  59.5 3.1 copy-start.19
  59.5 3.1 copy-start.20
  65.3 2.5 copy-start.7
  190.6 2.2 copy-start.10
  190.6 2.2 copy-start.22
  190.6 2.2 copy-start.24
  190.6 2.2 copy-start.26
  190.6 2.2 copy-start.28
  192.8 17.1 %copy-start = (bf16[4,42,8,1024]{3,2,0,1:T(8,128)(2,1)}, bf16[4,42,8,1024]{3,2,0,1:T(8,128)(2,1)S(1)}, u32[]{:S(2)}) copy-start(bf16[4,42,8,1024]{3,2,0,1:T(8,128)(2,1)S(1)} %copy.49) | copy-start | bytes 8257540
  193.0 11.3 %collective-permute-start.7 = (f32[1,512]{1,0:T(1,128)S(1)}, f32[1,512]{1,0:T(1,128)S(1)}, u32[]{:S(2)}, u32[]{:S(2)}) collective-permute-start(f32[1,512]{1,0:T(1,128)S(1)} %get-tuple-element.47), channel_id=1, source_target_pairs={{1,0},{2,1},{3,2},{4,3},{5,4},{6,5},{7,6},{9,8},{10,9},{11,10},{12... | collective-permute-start | bytes 6152 | tf_op jit(solution)/shard_map/ppermute | solution.py:303
  194.9 9.4 %collective-permute-start.6 = (f32[1,512]{1,0:T(1,128)S(1)}, f32[1,512]{1,0:T(1,128)S(1)}, u32[]{:S(2)}, u32[]{:S(2)}) collective-permute-start(f32[1,512]{1,0:T(1,128)S(1)} %get-tuple-element.46), channel_id=1, source_target_pairs={{0,1},{1,2},{2,3},{3,4},{4,5},{5,6},{6,7},{8,9},{9,10},{10,11},{11... | collective-permute-start | bytes 6152 | tf_op jit(solution)/shard_map/ppermute | solution.py:303
  197.4 8.5 %collective-permute-start.4 = (bf16[324,512]{1,0:T(8,128)(2,1)S(1)}, bf16[324,512]{1,0:T(8,128)(2,1)S(1)}, u32[]{:S(2)}, u32[]{:S(2)}) collective-permute-start(bf16[324,512]{1,0:T(8,128)(2,1)S(1)} %get-tuple-element.23), channel_id=1, source_target_pairs={{0,1},{1,2},{2,3},{3,4},{4,5},{5,6},{6,7},{8,9},{9,10},{10,11},{11... | collective-permute-start | bytes 995336 | tf_op jit(solution)/shard_map/ppermute | solution.py:303
  201.5 7.6 %collective-permute-start.5 = (bf16[324,512]{1,0:T(8,128)(2,1)S(1)}, bf16[324,512]{1,0:T(8,128)(2,1)S(1)}, u32[]{:S(2)}, u32[]{:S(2)}) collective-permute-start(bf16[324,512]{1,0:T(8,128)(2,1)S(1)} %get-tuple-element.22), channel_id=1, source_target_pairs={{1,0},{2,1},{3,2},{4,3},{5,4},{6,5},{7,6},{9,8},{10,9},{11,10},{12... | collective-permute-start | bytes 995336 | tf_op jit(solution)/shard_map/ppermute | solution.py:303
  330.4 3.0 copy-start.5

commit v2 on v1

v2 whole, which is shorter than its diff:
```python
import functools
import math

import jax
import jax.numpy as jnp
import numpy as np
from jax import lax
from jax.experimental import pallas as pl
from jax.experimental.pallas import tpu as pltpu
from jax.sharding import PartitionSpec as P

NDIR = 36
NFREQ = 36
K = NDIR * NFREQ
STEPS = 2

courant_scale = 0.5
current_scale = 0.15
source_step = 0.25
coriolis = 0.3
stress_scale = 0.5
drift_scale = 4.0

MESH = pl.DeviceIdType.MESH
F32 = jnp.float32
BF16 = jnp.bfloat16
VMEM_LIMIT = 60 * 1024 * 1024
ROWS = 16


def tap_table():
    component = np.arange(K)
    frequency = component // NDIR
    direction = component % NDIR
    angle = (direction + 0.5) * (2.0 * math.pi / NDIR)
    speed = courant_scale * np.exp(-2.0 * frequency / NFREQ)
    eastward = (4 * direction + 2 < NDIR) | (4 * direction + 2 > 3 * NDIR)
    northward = 2 * direction + 1 < NDIR
    forward = (1.0 / 6.0, -1.0, 0.5, 2.0 / 6.0, 0.0)
    backward = (0.0, -2.0 / 6.0, -0.5, 1.0, -1.0 / 6.0)
    columns = [speed * np.cos(angle), speed * np.sin(angle)]
    for mask in (eastward, northward):
        for f, b in zip(forward, backward):
            columns.append(np.where(mask, f, b))
    return np.stack(columns, 1).astype(np.float32)


def coupling_tables(layers):
    component = np.arange(K)
    frequency = component // NDIR
    angle = (component % NDIR + 0.5) * (2.0 * math.pi / NDIR)
    wavenum = 0.02 * np.exp(6.0 * frequency / NFREQ)
    depth = np.arange(layers)[:, None] + 0.5
    decay_rows = wavenum[None, :] ** 1.5 * np.exp(-2.0 * wavenum[None, :] * depth)
    decay_rows = decay_rows / np.sqrt(np.sum(decay_rows * decay_rows, axis=1, keepdims=True))
    drift_rows = drift_scale * np.concatenate(
        [decay_rows * np.cos(angle)[None, :], decay_rows * np.sin(angle)[None, :]], 0
    )
    stress = wavenum / np.sqrt(np.sum(wavenum * wavenum))
    stress_rows = -stress_scale * np.stack([stress * np.cos(angle), stress * np.sin(angle)], 0)
    return (drift_rows.astype(np.float32), stress_rows.astype(np.float32))


def pieces(rows):
    first = lax.reduce_precision(rows, 8, 7)
    rest = rows - first
    second = lax.reduce_precision(rest, 8, 7)
    third = rest - second
    return jnp.concatenate([first, second, third], 0).astype(BF16)


def constant_pieces(rows):
    first = rows.astype(BF16)
    rest = rows - first.astype(np.float32)
    second = rest.astype(BF16)
    third = (rest - second.astype(np.float32)).astype(BF16)
    return np.concatenate([first, second, third], 0)


def step_kernel(
    width, owners, inverse, state, land, place, rank, my_rank, taps, proj, outer, back, inner, velocity, mixing, active,
    out, new_velocity,
    field, east, north, drift, blocks, got, made, returned, pay, surface, surfaces,
    head, tail, before, after, east_head, east_tail, east_before, east_after,
    send_in, recv_in, send_back, recv_back, send_top, recv_top, send_edge, recv_edge,
):
    slots, chunks, comps, chunk_width = blocks.shape
    padded = field.shape[1]
    points = state.shape[1]
    block = points // slots
    block_rows = block // width
    rank_rows = back.shape[2]
    layers = mixing.shape[0]
    me = lax.axis_index("spec")
    strip = lax.axis_index("space")
    strips = lax.axis_size("space")
    edge = 2 * width
    has_before = strip > 0
    has_after = strip < strips - 1

    def peer(delta):
        return lax.rem(me + delta, slots)

    def spread_out(target, rows_at, low, value):
        for b in range(slots):
            start, stop = b * block, (b + 1) * block + 2 * edge
            first, last = max(start, low), min(stop, low + value.shape[1])
            if first < last:
                target[b, rows_at, first - start : last - start] = value[:, first - low : last - low]

    def copy(source, target, send, receive, device):
        return pltpu.make_async_remote_copy(
            src_ref=source, dst_ref=target, send_sem=send, recv_sem=receive,
            device_id=device, device_id_type=MESH,
        )

    def inward(j, delta):
        return copy(
            blocks.at[peer(delta), j], got.at[j, me],
            send_in.at[j, delta], recv_in.at[j, delta], {"spec": peer(delta)},
        )

    def homeward(j, delta):
        return copy(
            made.at[j, peer(delta)], returned.at[j, me],
            send_back.at[j, delta], recv_back.at[j, delta], {"spec": peer(delta)},
        )

    def upward(delta):
        return copy(
            surface, surfaces.at[me], send_top.at[delta], recv_top.at[delta], {"spec": peer(delta)}
        )

    def to_before(source, target, i):
        return copy(source, target, send_edge.at[i], recv_edge.at[i], {"space": strip - 1})

    def to_after(source, target, i):
        return copy(source, target, send_edge.at[i], recv_edge.at[i], {"space": strip + 1})

    barrier = pltpu.get_barrier_semaphore()
    for delta in range(1, slots):
        pl.semaphore_signal(
            barrier, inc=1, device_id={"spec": peer(delta)}, device_id_type=MESH
        )

    @pl.when(has_before)
    def _():
        pl.semaphore_signal(barrier, inc=1, device_id={"space": strip - 1}, device_id_type=MESH)

    @pl.when(has_after)
    def _():
        pl.semaphore_signal(barrier, inc=1, device_id={"space": strip + 1}, device_id_type=MESH)

    surface[0:1, :] = velocity[0, 0:1, :]
    surface[1:2, :] = velocity[1, 0:1, :]
    everywhere = jnp.concatenate([land[b] for b in range(slots)], 1)
    head[...] = (state[:, :edge].astype(F32) * everywhere[:, :edge]).astype(BF16)
    tail[...] = (state[:, points - edge :].astype(F32) * everywhere[:, points - edge :]).astype(BF16)
    expected = slots - 1 + has_before.astype(jnp.int32) + has_after.astype(jnp.int32)
    pl.semaphore_wait(barrier, expected)

    for delta in range(1, slots):
        upward(delta).start()

    @pl.when(has_before)
    def _():
        to_before(head, after, 0).start()

    @pl.when(has_after)
    def _():
        to_after(tail, before, 1).start()

    surfaces[me] = surface[...]
    whole_chunks = comps // ROWS
    rest = comps - whole_chunks * ROWS

    def fill(index, carry):
        here = pl.ds(pl.multiple_of(index * ROWS, ROWS), ROWS)
        masked = (state[here, :].astype(F32) * everywhere).astype(BF16)
        spread_out(field, here, edge, masked)
        return carry

    lax.fori_loop(0, whole_chunks, fill, 0)
    if rest:
        at = whole_chunks * ROWS
        for b in range(slots):
            field[b, at:, :] = jnp.zeros((padded - at, field.shape[2]), BF16)
        masked = (state[at:, :].astype(F32) * everywhere).astype(BF16)
        spread_out(field, slice(at, comps), edge, masked)

    for delta in range(1, slots):
        upward(delta).wait()
    currents = []
    for b in range(slots):
        here = jnp.zeros((2, block), F32)
        for s in range(slots):
            here = here + place[b, s] * surfaces[s]
        currents.append(here)
        north[b] = here[1:2]
    eastward = jnp.concatenate([here[0:1] for here in currents], 1)
    spread_out(east, slice(0, 1), edge, eastward)
    east_head[...] = eastward[:, :edge]
    east_tail[...] = eastward[:, points - edge :]

    @pl.when(has_before)
    def _():
        to_before(east_head, east_after, 2).start()

    @pl.when(has_after)
    def _():
        to_after(east_tail, east_before, 3).start()

    @pl.when(has_after)
    def _():
        to_after(head, after, 0).wait_recv()
        to_after(east_head, east_after, 2).wait_recv()
        spread_out(field, slice(0, comps), edge + points, after[...])
        spread_out(east, slice(0, 1), edge + points, east_after[...])

    @pl.when(jnp.logical_not(has_after))
    def _():
        spread_out(field, slice(0, comps), edge + points, jnp.zeros((comps, edge), BF16))
        spread_out(east, slice(0, 1), edge + points, jnp.zeros((1, edge), F32))

    @pl.when(has_before)
    def _():
        to_before(tail, before, 1).wait_recv()
        to_before(east_tail, east_before, 3).wait_recv()
        spread_out(field, slice(0, comps), 0, before[...])
        spread_out(east, slice(0, 1), 0, east_before[...])

    @pl.when(jnp.logical_not(has_before))
    def _():
        spread_out(field, slice(0, comps), 0, jnp.zeros((comps, edge), BF16))
        spread_out(east, slice(0, 1), 0, jnp.zeros((1, edge), F32))

    column = lax.broadcasted_iota(jnp.int32, (ROWS, width), 1)
    position = lax.broadcasted_iota(jnp.int32, (chunks * chunk_width, block), 0)

    def shifted(value, by):
        turned = pltpu.roll(value, by % width, 1)
        inside = (column >= by) if by > 0 else (column < width + by)
        return jnp.where(inside, turned, 0.0)

    def advect(b):
        def lanes(r):
            return slice(r * width, (r + 1) * width)

        def chunk(index, carry):
            here = pl.ds(pl.multiple_of(index * ROWS, ROWS), ROWS)
            tap = taps[here, :]

            def spread(i):
                return jnp.broadcast_to(tap[:, i : i + 1], (ROWS, width))

            speed_east, speed_north = spread(0), spread(1)
            row_tap = [spread(2 + i) for i in range(5)]
            col_tap = [spread(7 + i) for i in range(5)]
            masked = {}
            flow = {}
            for r in range(-2, block_rows + 2):
                masked[r] = field[b, here, lanes(r + 2)].astype(F32)
                flow[r] = (speed_east + current_scale * east[b, :, lanes(r + 2)]) * masked[r]
                c = r - 2
                if c < 0:
                    continue
                m = masked.pop(c)
                along = (speed_north + current_scale * north[b, :, lanes(c)]) * m
                total = m
                for i in range(5):
                    total = total - row_tap[i] * flow[c - 2 + i]
                total = total - col_tap[2] * along
                for i in (0, 1, 3, 4):
                    total = total - col_tap[i] * shifted(along, 2 - i)
                flow.pop(c - 2)
                drift[here, c * width : (c + 1) * width] = (total * land[b, :, lanes(c)]).astype(BF16)
            return carry

        lax.fori_loop(0, padded // ROWS, chunk, 0)
        spot = (position == rank[b]).astype(F32).astype(BF16)
        return lax.dot_general(
            drift[...], spot, (((1,), (1,)), ((), ())), preferred_element_type=F32
        ).astype(BF16)

    def one_slot(delta, carry):
        slot = peer(delta)
        packed = advect(owners[slot])

        for j in range(chunks):
            part = packed[:comps, j * chunk_width : (j + 1) * chunk_width]
            blocks[slot, j] = part

        @pl.when(delta < slots)
        def _():
            for j in range(chunks):
                inward(j, delta).start()

        return carry

    lax.fori_loop(1, slots + 1, one_slot, 0)
    for j in range(chunks):
        got[j, me] = blocks[me, j]

    def one_chunk(j, carry):
        for delta in range(1, slots):
            inward(j, delta).wait_recv()
        projected = jnp.dot(proj[0], got[j, 0], preferred_element_type=F32)
        for g in range(1, slots):
            projected = projected + jnp.dot(proj[g], got[j, g], preferred_element_type=F32)
        cubed = (projected * projected * projected).astype(BF16)
        for delta in list(range(1, slots)) + [0]:
            g = peer(delta)
            transfer = jnp.dot(back[g], cubed, preferred_element_type=F32)
            updated = (got[j, g].astype(F32) + source_step * transfer).astype(BF16)
            if delta:
                made[j, g] = updated
                homeward(j, delta).start()
            else:
                returned[j, g] = updated
        more = jnp.dot(inner[...], cubed, preferred_element_type=F32)
        for g in range(slots):
            more = more + jnp.dot(outer[g], got[j, g], preferred_element_type=F32)
        third = more.shape[0] // 3
        pay[j] = more[:third] + more[third : 2 * third] + more[2 * third :]
        return carry

    lax.fori_loop(0, chunks, one_chunk, 0)

    payload = None
    for j in range(chunks):
        spot = lax.broadcasted_iota(jnp.int32, (chunk_width, block), 0) + j * chunk_width
        spot = (spot == my_rank[...]).astype(F32).astype(BF16)
        value = pay[j]
        for _ in range(3):
            part = value.astype(BF16)
            value = value - part.astype(F32)
            term = jnp.dot(part, spot, preferred_element_type=F32)
            payload = term if payload is None else payload + term

    layer = lax.broadcasted_iota(jnp.int32, (layers, block), 0)
    depth = active[...]
    live = (layer < depth).astype(F32)
    bottom = (layer == depth - 1).astype(F32)
    top = (layer == 0).astype(F32)
    mix = mixing[...]
    upper = mix * ((layer + 1 < depth) & (layer < layers - 1)).astype(F32)

    def mixed(value):
        between = upper * (value - pltpu.roll(value, layers - 1, 0))
        return pltpu.roll(between, 1, 0) - between - mix * bottom * value

    old_east, old_north = velocity[0], velocity[1]
    drift_east = payload[:layers]
    drift_north = payload[layers : 2 * layers]
    stress_east = payload[2 * layers : 2 * layers + 1]
    stress_north = payload[2 * layers + 1 : 2 * layers + 2]
    new_velocity[0] = live * (
        old_east + coriolis * (old_north + drift_north) + mixed(old_east) + top * stress_east
    )
    new_velocity[1] = live * (
        old_north - coriolis * (old_east + drift_east) + mixed(old_north) + top * stress_north
    )

    for j in range(chunks):
        for delta in range(1, slots):
            homeward(j, delta).wait_recv()

    for b in range(slots):
        for j in range(chunks):
            spot = lax.broadcasted_iota(jnp.int32, (chunk_width, block), 0) + j * chunk_width
            spot = (spot == rank[b]).astype(F32).astype(BF16)
            term = jnp.dot(returned[j, inverse[b]], spot, preferred_element_type=F32)
            total = term if j == 0 else total + term
        out[:, b * block : (b + 1) * block] = total.astype(BF16)

    @pl.when(has_before)
    def _():
        to_before(head, after, 0).wait_send()
        to_before(east_head, east_after, 2).wait_send()

    @pl.when(has_after)
    def _():
        to_after(tail, before, 1).wait_send()
        to_after(east_tail, east_before, 3).wait_send()

    for j in range(chunks):
        for delta in range(1, slots):
            inward(j, delta).wait_send()
            homeward(j, delta).wait_send()


def whole(count, memory=pltpu.VMEM):
    return [pl.BlockSpec(memory_space=memory)] * count


def body(spectrum, land_sea, owners, proj_weight, back_weight, ocean_vel, mixing, active_layers):
    comps, rows, width = spectrum.shape
    slots = lax.axis_size("spec")
    points = rows * width
    block = points // slots
    cap = block * 3 // 4
    chunk_width = 256 if cap % 256 == 0 else cap
    chunks = cap // chunk_width
    layers = mixing.shape[0]
    rank_rows = proj_weight.shape[0]
    padded = -(-comps // ROWS) * ROWS
    edge = 2 * width
    me = lax.axis_index("spec")

    table = np.zeros((slots, padded, 12), np.float32)
    table[:, :comps] = tap_table().reshape(slots, comps, 12)
    taps = lax.dynamic_index_in_dim(jnp.asarray(table), me, 0, False)
    drift_rows, stress_rows = coupling_tables(layers)
    zeros = np.zeros((6, K), np.float32)
    outer = constant_pieces(np.concatenate([drift_rows, zeros, zeros[:2]], 0))
    outer = jnp.asarray(
        np.ascontiguousarray(outer.reshape(outer.shape[0], slots, comps).transpose(1, 0, 2))
    )
    through = jnp.dot(
        jnp.asarray(np.concatenate([source_step * drift_rows, stress_rows, zeros], 0)),
        back_weight.astype(F32),
        precision=lax.Precision.HIGHEST,
    )
    inner = pieces(through)
    proj = jnp.transpose(proj_weight.reshape(rank_rows, slots, comps), (1, 0, 2))
    back = back_weight.reshape(slots, comps, rank_rows)

    land = land_sea.astype(F32).reshape(slots, 1, block)
    covers = (owners[None, :] == jnp.arange(slots, dtype=jnp.int32)[:, None]).astype(jnp.int32)
    inverse = jnp.sum(covers * jnp.arange(slots, dtype=jnp.int32)[None], 1)
    place = jnp.broadcast_to(covers.astype(F32)[:, :, None, None], (slots, slots, 1, block))
    sea = land_sea.reshape(slots, block)
    rank = jnp.where(sea > 0, jnp.cumsum(sea, 1) - 1, -1).reshape(slots, 1, block)
    my_rank = lax.dynamic_index_in_dim(rank, owners[me], 0, False)

    velocity = ocean_vel.reshape(2, layers, block)
    mixing_local = mixing.reshape(layers, block)
    active = active_layers.reshape(1, block)
    state = spectrum.reshape(comps, points)
    pay_rows = inner.shape[0] // 3
    exchange = pltpu.VMEM((chunks, slots, comps, chunk_width), BF16)
    for _ in range(STEPS):
        state, velocity = pl.pallas_call(
            functools.partial(step_kernel, width),
            out_shape=(
                jax.ShapeDtypeStruct((comps, points), BF16),
                jax.ShapeDtypeStruct((2, layers, block), F32),
            ),
            in_specs=whole(2, pltpu.SMEM) + whole(13),
            out_specs=tuple(whole(2)),
            scratch_shapes=[
                pltpu.VMEM((slots, padded, block + 2 * edge), BF16),
                pltpu.VMEM((slots, 1, block + 2 * edge), F32),
                pltpu.VMEM((slots, 1, block), F32),
                pltpu.VMEM((padded, block), BF16),
                pltpu.VMEM((slots, chunks, comps, chunk_width), BF16),
                exchange,
                exchange,
                exchange,
                pltpu.VMEM((chunks, pay_rows, chunk_width), F32),
                pltpu.VMEM((2, block), F32),
                pltpu.VMEM((slots, 2, block), F32),
            ]
            + [pltpu.VMEM((comps, edge), BF16)] * 4
            + [pltpu.VMEM((1, edge), F32)] * 4
            + [pltpu.SemaphoreType.DMA((chunks, slots))] * 4
            + [pltpu.SemaphoreType.DMA((slots,))] * 2
            + [pltpu.SemaphoreType.DMA((4,))] * 2,
            compiler_params=pltpu.CompilerParams(
                vmem_limit_bytes=VMEM_LIMIT, collective_id=0, has_side_effects=True
            ),
            name="step",
        )(owners, inverse, state, land, place, rank, my_rank, taps, proj, outer, back, inner,
          velocity, mixing_local, active)
    return (state.reshape(comps, rows, width), velocity.reshape(ocean_vel.shape))


def solution(mesh):
    placed = (
        P("spec", "space", None),
        P("space", None),
        P(),
        P(),
        P(),
        P(None, None, "spec", "space", None),
        P(None, "spec", "space", None),
        P("spec", "space", None),
    )
    return jax.shard_map(
        body,
        mesh=mesh,
        in_specs=placed,
        out_specs=(P("spec", "space", None), P(None, None, "spec", "space", None)),
        check_vma=False,
    )
```

time: 336 us -> 253 us (0.75)
  starting transfers between devices: 20.6 us -> 0 us
  Pallas kernels: 235 us -> 216 us
  other arithmetic: 23.1 us -> 6.77 us
  blocking collectives: 13.4 us -> 0 us
  local copies, waits for them, and re-layouts: 33.9 us -> 20.6 us
  waiting for transfers between devices: 3.48 us -> 0 us
    ppermute x8 -> x0, starting transfers between devices: 20.6 us -> none  [shift_rows(): return (lax.ppermute(tail, 'space', up), lax.ppermute(head, 'space', down))]
    pallas_call x6 -> x2, Pallas kernels: 235 us -> 216 us  [body(): pl.pallas_call(functools.partial(step_kernel, width), out_shape=(jax.Shap...]
    all_gather x1 -> x0, blocking collectives: 13.4 us -> none  [body(): surfaces = lax.all_gather(velocity[:, 0], 'spec', axis=0)]
    pad x5 -> x0, local copies, waits for them, and re-layouts: 5.84 us -> none  [the longest x2 2.53 us: body(): after = jnp.pad(after, ((0, padded - comps), (0, 0)))]
    concatenate x3 -> x0, other arithmetic: 5.01 us -> none  [the longest x1 3.07 us: body(): proj = jnp.concatenate([proj_weight, outer_rows], 0)]
    slice x10 -> x1, local copies, waits for them, and re-layouts: 4.94 us -> 0.21 us  [the longest x2 4.07 us: body(): state[:comps].reshape(comps, rows, width)]
    reshape x5, local copies, waits for them, and re-layouts: 9.33 us -> 4.86 us  [the longest x2 1.84 us: body(): proj_weight.reshape(rank_rows, slots, comps)]
    ppermute x8 -> x0, waiting for transfers between devices: 3.48 us -> none  [shift_rows(): return (lax.ppermute(tail, 'space', up), lax.ppermute(head, 'space', down))]
  transfers between devices with their start and end apart: 8 -> 0, of which waited for: 2 -> 0; matrix products, arithmetic and copies ran while one was open for 12% -> 0% of each run, Pallas kernels for 0% -> 0%
where the time goes in v2:
time: 253 us; the launch traced here: 249 us
  Pallas kernels  216 us (85%)
  local copies, waits for them, and re-layouts  20.6 us (8%)
  other arithmetic  6.77 us (3%)
  between operations  2.65 us (1%)
    pallas_call x2, Pallas kernels, body(): pl.pallas_call(functools.partial(step_kernel, width), out_shape=(jax.Shap...  216 us
    unnamed x15, local copies, waits for them, and re-layouts  10.6 us

profile of v2, /device:TPU:2, one launch (start us, length us, event | category | flops | bytes accessed | tf_op | source)
XLA Modules:
  0.0 248.6 jit_solution(9572656359424869367)
XLA Ops:
  0.6 1.2 dynamic_slice.9
  3.8 1.3 select_reduce_fusion.inverse
  5.1 0.7 convert_convert_fusion
  5.7 0.7 broadcast_compare_fusion
  6.5 0.7 convert_element_type.19
  7.2 0.6 reshape.110.land
  7.8 0.7 reshape.111
  8.5 1.1 reduce-window.6
  9.7 0.2 slice_reduce_fusion
  9.9 0.2 reduce-window.9
  10.1 0.1 fusion.3
  10.1 0.1 add_add_fusion
  10.2 0.6 broadcast_select_fusion.rank
  10.9 0.0 copy-start.2
  10.9 0.6 dynamic-slice_select_fusion.my_rank
  11.5 0.7 broadcast_in_dim.3.place
  12.2 1.6 copy.26
  13.8 0.0 copy-start
  13.8 1.7 dynamic-slice_bitcast_fusion.taps
  15.5 2.3 reduce-precision_convert_fusion.1
  17.8 0.7 pad_maximum_fusion.inner
  18.5 0.0 copy-done.2
  18.5 0.0 copy-start.1
  18.5 0.8 copy.25
  19.3 0.0 copy-done
  19.3 1.3 reshape.114.back
  20.5 0.0 copy-done.1
  20.5 0.3 reshape.113
  20.8 1.6 copy.15
  22.4 1.9 pad.3
  24.3 2.8 %copy.19 = bf16[41,8,16,256]{3,1,2,0:T(8,128)(2,1)} copy(bf16[41,8,16,256]{3,2,1,0:T(8,128)(2,1)S(1)} %bitcast.31) | data formatting | bytes 5373952
  27.1 107.4 %step.2 = (bf16[324,4096]{1,0:T(8,128)(2,1)}, f32[2,32,1024]{2,1,0:T(8,128)}) custom-call(s32[4]{0:T(128)} %owners.3, s32[4]{0:T(128)} %select_reduce_fusion.inverse, bf16[324,4096]{1,0:T(8,128)(2,1)} %bitcast.32, f32[4,1,1024]{2,1,0:T(1,128)} %reshape.110.land, f32[4,4,1,1024]{3,2,1,0:T(1,128)} %broadcast_in_dim.3.place, ...), custom_call_target="tpu_custom_call" | custom-call | tf_op jit(solution)/shard_map/step/pallas_call | solution.py:443
  134.5 108.8 %step.3 = (bf16[324,4096]{1,0:T(8,128)(2,1)}, f32[2,32,1024]{2,1,0:T(8,128)}) custom-call(s32[4]{0:T(128)} %owners.3, s32[4]{0:T(128)} %select_reduce_fusion.inverse, bf16[324,4096]{1,0:T(8,128)(2,1)} %get-tuple-element.6.state, f32[4,1,1024]{2,1,0:T(1,128)} %reshape.110.land, f32[4,4,1,1024]{3,2,1,0:T(1,128)} %broadcast_in_dim.3.place, ...), custom_call_target="tpu_custom_call" | custom-call | tf_op jit(solution)/shard_map/step/pallas_call | solution.py:443
  243.3 2.6 %copy.21 = bf16[41,8,16,256]{3,2,1,0:T(8,128)(2,1)S(1)} copy(bf16[41,8,16,256]{3,1,2,0:T(8,128)(2,1)} %bitcast.34) | data formatting | bytes 5373952
  246.0 0.0 copy-start.3
  246.0 1.7 slice.9
  247.6 0.0 copy-done.3
  247.6 1.0 copy.16
  (3 shorter events, 0.0 us)
Async XLA Ops:
  10.9 7.7 %copy-start.2 = (f32[2,32,1,1,1024]{4,3,2,1,0:T(1,128)S(1)}, f32[2,32,1,1,1024]{4,3,2,1,0:T(1,128)}, u32[]{:S(2)}) copy-start(f32[2,32,1,1,1024]{4,3,2,1,0:T(1,128)} %param.16) | copy-start | bytes 786436
  13.8 5.5 %copy-start = (bf16[1296,512]{1,0:T(8,128)(2,1)S(1)}, bf16[1296,512]{1,0:T(8,128)(2,1)}, u32[]{:S(2)}) copy-start(bf16[1296,512]{1,0:T(8,128)(2,1)} %param.15) | copy-start | bytes 3981316
  18.5 2.0 copy-start.1
  246.0 1.7 copy-start.3

commit v3 on v2

--- a/solution.py
+++ b/solution.py
@@ -80,9 +80,10 @@
 def step_kernel(
     width, owners, inverse, state, land, place, rank, my_rank, taps, proj, outer, back, inner, velocity, mixing, active,
     out, new_velocity,
-    field, east, north, drift, blocks, got, made, returned, pay, surface, surfaces,
+    field, east, north, drift, blocks, got, made, returned, stage, pay, surface, surfaces,
     head, tail, before, after, east_head, east_tail, east_before, east_after,
     send_in, recv_in, send_back, recv_back, send_top, recv_top, send_edge, recv_edge,
+    *relay
 ):
     slots, chunks, comps, chunk_width = blocks.shape
     padded = field.shape[1]
@@ -125,6 +126,55 @@
             made.at[j, peer(delta)], returned.at[j, me],
             send_back.at[j, delta], recv_back.at[j, delta], {"spec": peer(delta)},
         )
+
+    if relay:
+        (cube, cubes, moved, landed, send_cube, recv_cube, send_moved, recv_moved) = relay
+        half = me // 2
+        mate = me + 1 - 2 * (me % 2)
+        other = 2 - 2 * half
+        hub = 2 - half
+        inner_device = (me == 1) | (me == 2)
+
+    def to_mate(j):
+        return copy(
+            made.at[j, mate], returned.at[j, me],
+            send_back.at[j, 0], recv_back.at[j, 0], {"spec": mate},
+        )
+
+    def to_hub(j):
+        return copy(
+            cube.at[j], cubes.at[j, me % 2],
+            send_cube.at[j], recv_cube.at[j, me % 2], {"spec": hub},
+        )
+
+    def from_owner(j, k):
+        return copy(cube.at[j], cubes.at[j, k], send_cube.at[j], recv_cube.at[j, k], {"spec": hub})
+
+    def onward(j, k):
+        return copy(
+            moved.at[j, k], landed.at[j, k],
+            send_moved.at[j, k], recv_moved.at[j, k], {"spec": mate},
+        )
+
+    def pass_on(j):
+        for k in range(2):
+            from_owner(j, k).wait_recv()
+            moved[j, k] = jnp.dot(
+                back[mate], cubes[j, k], preferred_element_type=F32
+            ).astype(BF16)
+            onward(j, k).start()
+        for k in range(2):
+            transfer = jnp.dot(back[me], cubes[j, k], preferred_element_type=F32)
+            returned[j, other + k] = (
+                blocks[other + k, j].astype(F32) + source_step * transfer
+            ).astype(BF16)
+
+    def take_in(j):
+        for k in range(2):
+            onward(j, k).wait_recv()
+            returned[j, other + k] = (
+                blocks[other + k, j].astype(F32) + source_step * landed[j, k].astype(F32)
+            ).astype(BF16)
 
     def upward(delta):
         return copy(
@@ -308,13 +358,18 @@
         for g in range(1, slots):
             projected = projected + jnp.dot(proj[g], got[j, g], preferred_element_type=F32)
         cubed = (projected * projected * projected).astype(BF16)
-        for delta in list(range(1, slots)) + [0]:
-            g = peer(delta)
+        if relay:
+            cube[j] = cubed
+            to_hub(j).start()
+            targets = [(mate, 1), (me, 0)]
+        else:
+            targets = [(peer(delta), delta) for delta in list(range(1, slots)) + [0]]
+        for g, delta in targets:
             transfer = jnp.dot(back[g], cubed, preferred_element_type=F32)
             updated = (got[j, g].astype(F32) + source_step * transfer).astype(BF16)
             if delta:
                 made[j, g] = updated
-                homeward(j, delta).start()
+                (to_mate(j) if relay else homeward(j, delta)).start()
             else:
                 returned[j, g] = updated
         more = jnp.dot(inner[...], cubed, preferred_element_type=F32)
@@ -322,9 +377,21 @@
             more = more + jnp.dot(outer[g], got[j, g], preferred_element_type=F32)
         third = more.shape[0] // 3
         pay[j] = more[:third] + more[third : 2 * third] + more[2 * third :]
+        if relay:
+
+            @pl.when(inner_device & (j > 0))
+            def _():
+                pass_on(jnp.maximum(j - 1, 0))
+
         return carry
 
     lax.fori_loop(0, chunks, one_chunk, 0)
+    if relay:
+
+        @pl.when(inner_device)
+        def _():
+            pass_on(chunks - 1)
+
 
     payload = None
     for j in range(chunks):
@@ -361,17 +428,38 @@
         old_north - coriolis * (old_east + drift_east) + mixed(old_north) + top * stress_north
     )
 
-    for j in range(chunks):
-        for delta in range(1, slots):
-            homeward(j, delta).wait_recv()
-
-    for b in range(slots):
-        for j in range(chunks):
-            spot = lax.broadcasted_iota(jnp.int32, (chunk_width, block), 0) + j * chunk_width
-            spot = (spot == rank[b]).astype(F32).astype(BF16)
-            term = jnp.dot(returned[j, inverse[b]], spot, preferred_element_type=F32)
-            total = term if j == 0 else total + term
-        out[:, b * block : (b + 1) * block] = total.astype(BF16)
+    def expand(j, carry):
+        if relay:
+            to_mate(j).wait_recv()
+
+            @pl.when(jnp.logical_not(inner_device))
+            def _():
+                take_in(j)
+
+        else:
+            for delta in range(1, slots):
+                homeward(j, delta).wait_recv()
+        for s in range(slots):
+            stage[s] = returned[j, s]
+        spot = lax.broadcasted_iota(jnp.int32, (chunk_width, block), 0) + j * chunk_width
+        for b in range(slots):
+            at = slice(b * block, (b + 1) * block)
+            here = (spot == rank[b]).astype(F32).astype(BF16)
+            term = jnp.dot(
+                stage[inverse[b]], here, preferred_element_type=F32
+            ).astype(BF16)
+
+            @pl.when(j == 0)
+            def _():
+                out[:, at] = term
+
+            @pl.when(j > 0)
+            def _():
+                out[:, at] = out[:, at] + term
+
+        return carry
+
+    lax.fori_loop(0, chunks, expand, 0)
 
     @pl.when(has_before)
     def _():
@@ -386,7 +474,18 @@
     for j in range(chunks):
         for delta in range(1, slots):
             inward(j, delta).wait_send()
-            homeward(j, delta).wait_send()
+            if not relay:
+                homeward(j, delta).wait_send()
+        if relay:
+            to_mate(j).wait_send()
+            to_hub(j).wait_send()
+    if relay:
+
+        @pl.when(inner_device)
+        def _():
+            for j in range(chunks):
+                for k in range(2):
+                    onward(j, k).wait_send()
 
 
 def whole(count, memory=pltpu.VMEM):
@@ -439,6 +538,15 @@
     state = spectrum.reshape(comps, points)
     pay_rows = inner.shape[0] // 3
     exchange = pltpu.VMEM((chunks, slots, comps, chunk_width), BF16)
+    relay = []
+    if slots == 4:
+        pair = pltpu.VMEM((chunks, 2, comps, chunk_width), BF16)
+        both = pltpu.SemaphoreType.DMA((chunks, 2))
+        relay = [
+            pltpu.VMEM((chunks, rank_rows, chunk_width), BF16),
+            pltpu.VMEM((chunks, 2, rank_rows, chunk_width), BF16),
+            pair, pair, pltpu.SemaphoreType.DMA((chunks,)), both, both, both,
+        ]
     for _ in range(STEPS):
         state, velocity = pl.pallas_call(
             functools.partial(step_kernel, width),
@@ -457,6 +565,7 @@
                 exchange,
                 exchange,
                 exchange,
+                pltpu.VMEM((slots, comps, chunk_width), BF16),
                 pltpu.VMEM((chunks, pay_rows, chunk_width), F32),
                 pltpu.VMEM((2, block), F32),
                 pltpu.VMEM((slots, 2, block), F32),
@@ -465,7 +574,8 @@
             + [pltpu.VMEM((1, edge), F32)] * 4
             + [pltpu.SemaphoreType.DMA((chunks, slots))] * 4
             + [pltpu.SemaphoreType.DMA((slots,))] * 2
-            + [pltpu.SemaphoreType.DMA((4,))] * 2,
+            + [pltpu.SemaphoreType.DMA((4,))] * 2
+            + relay,
             compiler_params=pltpu.CompilerParams(
                 vmem_limit_bytes=VMEM_LIMIT, collective_id=0, has_side_effects=True
             ),

time: 253 us -> 253 us (level)
  no operation moved by 1% of the time
where the time goes in v3:
time: 253 us; the launch traced here: 249 us
  Pallas kernels  217 us (86%)
  local copies, waits for them, and re-layouts  20.6 us (8%)
  other arithmetic  6.77 us (3%)
  between operations  2.65 us (1%)
    pallas_call x2, Pallas kernels, body(): pl.pallas_call(functools.partial(step_kernel, width), out_shape=(jax.Shap...  217 us
    unnamed x15, local copies, waits for them, and re-layouts  10.6 us

profile of v3, /device:TPU:2, one launch (start us, length us, event | category | flops | bytes accessed | tf_op | source)
XLA Modules:
  0.0 249.4 jit_solution(4976317228979252663)
XLA Ops:
  0.6 1.2 dynamic_slice.9
  3.8 1.3 select_reduce_fusion.inverse
  5.1 0.7 convert_convert_fusion
  5.7 0.7 broadcast_compare_fusion
  6.5 0.7 convert_element_type.19
  7.2 0.6 reshape.110.land
  7.8 0.7 reshape.111
  8.5 1.1 reduce-window.6
  9.7 0.2 slice_reduce_fusion
  9.9 0.2 reduce-window.9
  10.1 0.1 fusion.3
  10.1 0.1 add_add_fusion
  10.2 0.6 broadcast_select_fusion.rank
  10.9 0.0 copy-start.2
  10.9 0.6 dynamic-slice_select_fusion.my_rank
  11.5 0.7 broadcast_in_dim.3.place
  12.2 1.6 copy.26
  13.8 0.0 copy-start
  13.8 1.7 dynamic-slice_bitcast_fusion.taps
  15.5 2.3 reduce-precision_convert_fusion.1
  17.8 0.7 pad_maximum_fusion.inner
  18.5 0.0 copy-done.2
  18.5 0.0 copy-start.1
  18.5 0.8 copy.25
  19.3 0.0 copy-done
  19.3 1.3 reshape.114.back
  20.5 0.0 copy-done.1
  20.5 0.3 reshape.113
  20.8 1.6 copy.15
  22.4 1.9 pad.3
  24.3 2.8 %copy.19 = bf16[41,8,16,256]{3,1,2,0:T(8,128)(2,1)} copy(bf16[41,8,16,256]{3,2,1,0:T(8,128)(2,1)S(1)} %bitcast.31) | data formatting | bytes 5373952
  27.1 109.3 %step.2 = (bf16[324,4096]{1,0:T(8,128)(2,1)}, f32[2,32,1024]{2,1,0:T(8,128)}) custom-call(s32[4]{0:T(128)} %owners.3, s32[4]{0:T(128)} %select_reduce_fusion.inverse, bf16[324,4096]{1,0:T(8,128)(2,1)} %bitcast.32, f32[4,1,1024]{2,1,0:T(1,128)} %reshape.110.land, f32[4,4,1,1024]{3,2,1,0:T(1,128)} %broadcast_in_dim.3.place, ...), custom_call_target="tpu_custom_call" | custom-call | tf_op jit(solution)/shard_map/step/pallas_call | solution.py:551
  136.4 107.7 %step.3 = (bf16[324,4096]{1,0:T(8,128)(2,1)}, f32[2,32,1024]{2,1,0:T(8,128)}) custom-call(s32[4]{0:T(128)} %owners.3, s32[4]{0:T(128)} %select_reduce_fusion.inverse, bf16[324,4096]{1,0:T(8,128)(2,1)} %get-tuple-element.6.state, f32[4,1,1024]{2,1,0:T(1,128)} %reshape.110.land, f32[4,4,1,1024]{3,2,1,0:T(1,128)} %broadcast_in_dim.3.place, ...), custom_call_target="tpu_custom_call" | custom-call | tf_op jit(solution)/shard_map/step/pallas_call | solution.py:551
  244.2 2.6 %copy.21 = bf16[41,8,16,256]{3,2,1,0:T(8,128)(2,1)S(1)} copy(bf16[41,8,16,256]{3,1,2,0:T(8,128)(2,1)} %bitcast.34) | data formatting | bytes 5373952
  246.8 0.0 copy-start.3
  246.8 1.7 slice.9
  248.5 0.0 copy-done.3
  248.5 1.0 copy.16
  (3 shorter events, 0.0 us)
Async XLA Ops:
  10.9 7.7 %copy-start.2 = (f32[2,32,1,1,1024]{4,3,2,1,0:T(1,128)S(1)}, f32[2,32,1,1,1024]{4,3,2,1,0:T(1,128)}, u32[]{:S(2)}) copy-start(f32[2,32,1,1,1024]{4,3,2,1,0:T(1,128)} %param.16) | copy-start | bytes 786436
  13.8 5.5 %copy-start = (bf16[1296,512]{1,0:T(8,128)(2,1)S(1)}, bf16[1296,512]{1,0:T(8,128)(2,1)}, u32[]{:S(2)}) copy-start(bf16[1296,512]{1,0:T(8,128)(2,1)} %param.15) | copy-start | bytes 3981316
  18.5 2.0 copy-start.1
  246.8 1.7 copy-start.3

commit v4 on v3

--- a/solution.py
+++ b/solution.py
@@ -539,14 +539,6 @@
     pay_rows = inner.shape[0] // 3
     exchange = pltpu.VMEM((chunks, slots, comps, chunk_width), BF16)
     relay = []
-    if slots == 4:
-        pair = pltpu.VMEM((chunks, 2, comps, chunk_width), BF16)
-        both = pltpu.SemaphoreType.DMA((chunks, 2))
-        relay = [
-            pltpu.VMEM((chunks, rank_rows, chunk_width), BF16),
-            pltpu.VMEM((chunks, 2, rank_rows, chunk_width), BF16),
-            pair, pair, pltpu.SemaphoreType.DMA((chunks,)), both, both, both,
-        ]
     for _ in range(STEPS):
         state, velocity = pl.pallas_call(
             functools.partial(step_kernel, width),

time: 253 us -> 252 us (level)
  no operation moved by 1% of the time
where the time goes in v4:
time: 252 us; the launch traced here: 248 us
  Pallas kernels  215 us (85%)
  local copies, waits for them, and re-layouts  20.6 us (8%)
  other arithmetic  6.77 us (3%)
  between operations  2.65 us (1%)
    pallas_call x2, Pallas kernels, body(): pl.pallas_call(functools.partial(step_kernel, width), out_shape=(jax.Shap...  215 us
    unnamed x15, local copies, waits for them, and re-layouts  10.6 us

profile of v4, /device:TPU:2, one launch (start us, length us, event | category | flops | bytes accessed | tf_op | source)
XLA Modules:
  0.0 247.5 jit_solution(1129075457137687206)
XLA Ops:
  0.6 1.2 dynamic_slice.9
  3.8 1.3 select_reduce_fusion.inverse
  5.1 0.7 convert_convert_fusion
  5.7 0.7 broadcast_compare_fusion
  6.5 0.7 convert_element_type.19
  7.2 0.6 reshape.110.land
  7.8 0.7 reshape.111
  8.5 1.1 reduce-window.6
  9.7 0.2 slice_reduce_fusion
  9.9 0.2 reduce-window.9
  10.1 0.1 fusion.3
  10.1 0.1 add_add_fusion
  10.2 0.6 broadcast_select_fusion.rank
  10.9 0.0 copy-start.2
  10.9 0.6 dynamic-slice_select_fusion.my_rank
  11.5 0.7 broadcast_in_dim.3.place
  12.2 1.6 copy.26
  13.8 0.0 copy-start
  13.8 1.7 dynamic-slice_bitcast_fusion.taps
  15.5 2.3 reduce-precision_convert_fusion.1
  17.8 0.7 pad_maximum_fusion.inner
  18.5 0.0 copy-done.2
  18.5 0.0 copy-start.1
  18.5 0.8 copy.25
  19.3 0.0 copy-done
  19.3 1.3 reshape.114.back
  20.5 0.0 copy-done.1
  20.5 0.3 reshape.113
  20.8 1.6 copy.15
  22.4 1.9 pad.3
  24.3 2.8 %copy.19 = bf16[41,8,16,256]{3,1,2,0:T(8,128)(2,1)} copy(bf16[41,8,16,256]{3,2,1,0:T(8,128)(2,1)S(1)} %bitcast.31) | data formatting | bytes 5373952
  27.1 106.9 %step.2 = (bf16[324,4096]{1,0:T(8,128)(2,1)}, f32[2,32,1024]{2,1,0:T(8,128)}) custom-call(s32[4]{0:T(128)} %owners.3, s32[4]{0:T(128)} %select_reduce_fusion.inverse, bf16[324,4096]{1,0:T(8,128)(2,1)} %bitcast.32, f32[4,1,1024]{2,1,0:T(1,128)} %reshape.110.land, f32[4,4,1,1024]{3,2,1,0:T(1,128)} %broadcast_in_dim.3.place, ...), custom_call_target="tpu_custom_call" | custom-call | tf_op jit(solution)/shard_map/step/pallas_call | solution.py:543
  134.0 108.3 %step.3 = (bf16[324,4096]{1,0:T(8,128)(2,1)}, f32[2,32,1024]{2,1,0:T(8,128)}) custom-call(s32[4]{0:T(128)} %owners.3, s32[4]{0:T(128)} %select_reduce_fusion.inverse, bf16[324,4096]{1,0:T(8,128)(2,1)} %get-tuple-element.6.state, f32[4,1,1024]{2,1,0:T(1,128)} %reshape.110.land, f32[4,4,1,1024]{3,2,1,0:T(1,128)} %broadcast_in_dim.3.place, ...), custom_call_target="tpu_custom_call" | custom-call | tf_op jit(solution)/shard_map/step/pallas_call | solution.py:543
  242.2 2.6 %copy.21 = bf16[41,8,16,256]{3,2,1,0:T(8,128)(2,1)S(1)} copy(bf16[41,8,16,256]{3,1,2,0:T(8,128)(2,1)} %bitcast.34) | data formatting | bytes 5373952
  244.9 0.0 copy-start.3
  244.9 1.7 slice.9
  246.5 0.0 copy-done.3
  246.6 1.0 copy.16
  (3 shorter events, 0.0 us)
Async XLA Ops:
  10.9 7.7 %copy-start.2 = (f32[2,32,1,1,1024]{4,3,2,1,0:T(1,128)S(1)}, f32[2,32,1,1,1024]{4,3,2,1,0:T(1,128)}, u32[]{:S(2)}) copy-start(f32[2,32,1,1,1024]{4,3,2,1,0:T(1,128)} %param.16) | copy-start | bytes 786436
  13.8 5.5 %copy-start = (bf16[1296,512]{1,0:T(8,128)(2,1)S(1)}, bf16[1296,512]{1,0:T(8,128)(2,1)}, u32[]{:S(2)}) copy-start(bf16[1296,512]{1,0:T(8,128)(2,1)} %param.15) | copy-start | bytes 3981316
  18.5 2.0 copy-start.1
  244.9 1.7 copy-start.3
